TPU v7x, 512 devices: a whole 4x4x16 slice. The times are simulated.
512 devices in a mesh: dp: 8 (over y, z_hi), rows: 64 (over z_lo, x, core).
Axes of the slice: x: 4, y: 4, z: 16 (z_hi: 2, z_lo: 8; z = z_hi * 8 + z_lo), core: 2. Of those that a mesh axis runs over, the one named last changes fastest.
Arguments:
- features: bfloat16 [8, 256, 256, 128], P('dp', 'rows'), may hold values from -6 to 6
- conv_weight: bfloat16 [3, 3, 128, 128], replicated, may hold values from -0.1875 to 0.1875
- out_weight: bfloat16 [128, 3], replicated, may hold values from -0.5 to 0.5
- targets: float32 [8, 256, 256, 3], P('dp', 'rows'), may hold values from -4 to 4
- disc_weight: float32 [3, 3, 3, 64], replicated, may hold values from -1.25 to 1.25
- disc_head: float32 [64], replicated, may hold values from -0.75 to 0.75
- lpips_weight: float32 [3, 3, 3, 64], replicated, may hold values from -1.25 to 1.25
- lpips_lin: float32 [64], replicated, may hold values from 0.1 to 1
Outputs:
- recon: float32 [8, 256, 256, 3], P('dp', 'rows')
- grad_features: bfloat16 [8, 256, 256, 128], P('dp', 'rows')
- grad_conv: float32 [3, 3, 128, 128], P(None, None, None, 'dp')
- grad_out: float32 [128, 3], P('dp')
All inputs are finite; a program needn't handle non-finite values.
Results may differ from a plain program's by a relative error of at most 0.01.
Values may be sent and summed in bfloat16 or wider, within the bound.
No kernel may reach another device: no remote copies, remote signals or barrier semaphores. Data moves between devices by JAX's collectives and lax.ppermute only.
A program may use at most 64 MiB of HBM per device.

v0:
```python
import jax
import jax.numpy as jnp
from jax import lax
from jax.sharding import PartitionSpec as P

adv_scale = 0.5
charb_eps = 0.01


def padded_2(cells, sides, width):
    for axis, dim in sides:
        count = lax.axis_size(axis)
        ends = count - 1
        head = lax.slice_in_dim(cells, 0, width, axis=dim)
        tail = lax.slice_in_dim(cells, cells.shape[dim] - width, cells.shape[dim], axis=dim)
        cells = jnp.concatenate(
            [
                lax.ppermute(tail, axis, [(i, (i + 1) % count) for i in range(ends)]),
                cells,
                lax.ppermute(head, axis, [((i + 1) % count, i) for i in range(ends)]),
            ],
            axis=dim,
        )
    return cells


def in_blocks(array, dim, peers):
    dims = array.shape
    tiles = array.reshape(*dims[:dim], peers, dims[dim] // peers, *dims[dim + 1 :])
    return jnp.moveaxis(tiles, dim, 0)


def sent_and_summed(array, axis, dim):
    tiles = in_blocks(array, dim, lax.axis_size(axis))
    arrived = lax.all_to_all(tiles, axis, split_axis=0, concat_axis=0, tiled=True)
    return arrived.astype(jnp.float32).sum(axis=0)


def over_pieces(array, axis):
    tiles = lax.all_gather(array, axis)
    return tiles.sum(axis=0)


def convolve(inputs, kernel, padding, precision):
    return lax.conv_general_dilated(
        inputs,
        kernel,
        (1, 1),
        padding,
        dimension_numbers=("NHWC", "HWIO", "NHWC"),
        preferred_element_type=jnp.float32,
        precision=precision,
    )


def leaky_smooth(values):
    return 0.2 * values + 0.8 * jax.nn.softplus(values)


def tile_loss(images, truth, disc_weight, disc_head, lpips_weight, lpips_lin, divisor, row_valid):
    high = lax.Precision.DEFAULT
    side = ((0, 0), (1, 1))
    differ_img = images[:, 2:-2] - truth[:, 2:-2]
    recon_term = jnp.sum(jnp.sqrt(differ_img * differ_img + charb_eps))
    disc = leaky_smooth(convolve(images, disc_weight, side, high))
    logits = jnp.einsum("nhwc,c->nhw", disc, disc_head, precision=high)
    feats_a = jax.nn.gelu(convolve(images, lpips_weight, side, high), approximate=True)
    feats_b = jax.nn.gelu(convolve(truth, lpips_weight, side, high), approximate=True)
    norm_a = feats_a * lax.rsqrt(jnp.mean(feats_a * feats_a, axis=-1, keepdims=True) + 1e-06)
    norm_b = feats_b * lax.rsqrt(jnp.mean(feats_b * feats_b, axis=-1, keepdims=True) + 1e-06)
    differ = norm_a - norm_b
    percep = jnp.sum(differ * differ * lpips_lin * row_valid)
    return (recon_term - adv_scale * jnp.sum(logits * row_valid[..., 0]) + percep) / divisor


def weight_taps(padded, grad_pre, rows_loc, cols_loc):
    width = grad_pre.shape[-1]
    flat_grad = grad_pre.reshape(-1, width)
    result = []
    for row_tap in range(3):
        line = []
        for col_tap in range(3):
            window = padded[
                :, row_tap : row_tap + rows_loc, col_tap : col_tap + cols_loc, :
            ].reshape(-1, padded.shape[-1])
            line.append(
                lax.dot_general(
                    window, flat_grad, (((0,), (0,)), ((), ())), preferred_element_type=jnp.float32
                )
            )
        result.append(jnp.stack(line))
    return jnp.stack(result)


def body(
    features, conv_weight, out_weight, targets, disc_weight, disc_head, lpips_weight, lpips_lin
):
    high = lax.Precision.DEFAULT
    frames, rows_loc, cols, width = features.shape
    height = rows_loc * lax.axis_size("rows")
    first_row = lax.axis_index("rows") * rows_loc
    side = ((0, 0), (1, 1))

    def row_mask(offset, count):
        global_rows = first_row + offset + jnp.arange(count, dtype=jnp.int32)
        inside = jnp.logical_and(global_rows >= 0, global_rows < height)
        return inside.astype(jnp.float32)[None, :, None, None]

    deep = padded_2(features, (("rows", 1),), 3)
    wide_pre = convolve(deep, conv_weight, side, None)
    wide_hidden = jax.nn.silu(wide_pre).astype(jnp.bfloat16)
    wide_recon = jnp.dot(
        wide_hidden.reshape(-1, width), out_weight, preferred_element_type=jnp.float32
    ).reshape(frames, rows_loc + 4, cols, 3)
    wide_recon = wide_recon * row_mask(-2, rows_loc + 4)
    wide_truth = padded_2(targets, (("rows", 1),), 2)
    rimmed = deep[:, 2:-2]
    preact = wide_pre[:, 2:-2]
    hidden = wide_hidden[:, 2:-2]
    flat_hidden = hidden.reshape(-1, width)
    recon = wide_recon[:, 2:-2]
    row_valid = row_mask(-1, rows_loc + 2)
    grad_wide = jax.grad(tile_loss)(
        wide_recon, wide_truth, disc_weight, disc_head, lpips_weight, lpips_lin, frames, row_valid
    )
    grad_image = grad_wide[:, 2 : 2 + rows_loc]
    flat_img = grad_image.reshape(-1, 3)
    grad_hidden = jnp.dot(flat_img, out_weight.astype(jnp.float32).T, precision=high).reshape(
        preact.shape
    )
    sigma = jax.nn.sigmoid(preact)
    grad_pre = (grad_hidden * sigma * (1.0 + preact * (1.0 - sigma))).astype(jnp.bfloat16)
    grad_rimmed = padded_2(grad_pre, (("rows", 1),), 1)
    flipped = jnp.transpose(conv_weight[::-1, ::-1], (0, 1, 3, 2))
    grad_features = convolve(grad_rimmed, flipped, side, None).astype(jnp.bfloat16)
    padded = jnp.pad(rimmed, ((0, 0), (0, 0), (1, 1), (0, 0)))
    local_conv = weight_taps(padded, grad_pre, rows_loc, cols)
    local_out = jnp.dot(flat_hidden.astype(jnp.float32).T, flat_img, precision=high)
    kept_conv, kept_out = (
        sent_and_summed(local_conv.astype(jnp.bfloat16), "dp", 3),
        sent_and_summed(local_out.astype(jnp.bfloat16), "dp", 0),
    )
    grad_conv, grad_out = (over_pieces(kept_conv, "rows"), over_pieces(kept_out, "rows"))
    return (recon, grad_features, grad_conv, grad_out)


def solution(mesh):
    in_specs = (
        P("dp", "rows", None, None),
        P(),
        P(),
        P("dp", "rows", None, None),
        P(),
        P(),
        P(),
        P(),
    )
    out_specs = (
        P("dp", "rows", None, None),
        P("dp", "rows", None, None),
        P(None, None, None, "dp"),
        P("dp", None),
    )
    return jax.shard_map(body, mesh=mesh, in_specs=in_specs, out_specs=out_specs, check_vma=False)
```

profile of v0, /device:TPU:1, one launch (start us, length us, event | category | flops | bytes accessed | tf_op | source)
XLA Modules:
  0.0 278.7 jit_solution(13932795147019351933)
XLA Ops:
  7.3 0.8 fusion.153
  8.0 4.5 %collective-permute-start.2 = (bf16[1,2,256,3]{2,1,3,0:T(2,128)(2,1)S(1)}, bf16[1,2,256,3]{2,1,3,0:T(2,128)(2,1)S(1)}, u32[]{:S(2)}, u32[]{:S(2)}) collective-permute-start(bf16[1,2,256,3]{2,1,3,0:T(2,128)(2,1)S(1)} %get-tuple-element.35), channel_id=1, source_target_pairs={{0,1},{1,2},{2,3},{3,4},{4,5},{5,6},{6,7},{7,8},{8,9},{9,10},{10,1... | collective-permute-start | bytes 9224 | tf_op jit(solution)/shard_map/ppermute | solution.py:18
  12.5 5.5 %collective-permute-start.3 = (bf16[1,2,256,3]{2,1,3,0:T(2,128)(2,1)S(1)}, bf16[1,2,256,3]{2,1,3,0:T(2,128)(2,1)S(1)}, u32[]{:S(2)}, u32[]{:S(2)}) collective-permute-start(bf16[1,2,256,3]{2,1,3,0:T(2,128)(2,1)S(1)} %get-tuple-element.36), channel_id=1, source_target_pairs={{1,0},{2,1},{3,2},{4,3},{5,4},{6,5},{7,6},{8,7},{9,8},{10,9},{11,1... | collective-permute-start | bytes 9224 | tf_op jit(solution)/shard_map/ppermute | solution.py:20
  18.1 1.1 copy.142
  19.2 1.9 collective-permute-start
  21.1 3.1 %collective-permute-start.1 = (bf16[1,3,256,128]{2,3,1,0:T(8,128)(2,1)S(1)}, bf16[1,3,256,128]{2,3,1,0:T(8,128)(2,1)}, u32[]{:S(2)}, u32[]{:S(2)}) collective-permute-start(bf16[1,3,256,128]{2,3,1,0:T(8,128)(2,1)S(1)} %get-tuple-element.32), channel_id=1, source_target_pairs={{1,0},{2,1},{3,2},{4,3},{5,4},{6,5},{7,6},{8,7},{9,8},{10,9},{11,1... | collective-permute-start | bytes 589832 | tf_op jit(solution)/shard_map/ppermute | solution.py:20
  26.4 1.9 fusion.154
  28.6 1.3 copy.157
  29.9 0.9 slice_reduce_fusion
  30.8 1.1 pad_maximum_fusion
  33.4 1.6 multiply_convert_fusion
  35.3 0.9 slice.131
  37.3 0.6 add_multiply_fusion.1
  38.5 0.8 slice.132
  39.3 3.3 %fusion.150 = (f32[6,8,33,64]{3,1,2,0:T(8,128)}, f32[6,8,33,64]{3,1,2,0:T(8,128)}, f32[6,8,33,64]{3,1,2,0:T(8,128)}, f32[6,8,33,64]{3,1,2,0:T(8,128)}, f32[6,8,33,64]{3,1,2,0:T(8,128)}, /*index=5*/f32[6,8,33,64]{3,1,2,0:T(8,128)}) fusion(f32[3,3,3,64]{3,2,1,0:T(4,128)S(1)} %copy-done.20, bf16[8,1,7,2,3]{2,4,3,0,1:T(4,128)(2,1)S(1)} %slice.115, ...), kind=kOutput, calls=%fused_computation.213 | convolution fusion | flops 6832512 | bytes 2453544 | tf_op jit(solution)/shard_map/jvp()/conv_general_dilated | solution.py:45
  42.6 1.3 fusion.45
  44.2 0.8 fusion.49
  45.7 10.6 %convolution_select_fusion.5 = f32[8,8,33,3]{1,3,2,0:T(4,128)} fusion(f32[3,3,3,64]{3,2,1,0:T(4,128)S(1)} %copy-done.18, bf16[6,1,7,2,64]{4,2,3,0,1:T(8,128)(2,1)S(1)} %slice.127, bf16[6,1,8,33,64]{4,2,3,0,1:T(8,128)(2,1)S(1)} %copy.167, pred[8,33]{0,1:T(8,128)(4,1)S(1)} %copy-done.24), kind=kOutput, calls=%fused_computation.10 | convolution fusion | flops 6125760 | bytes 246024 | tf_op jit(solution)/shard_map/transpose(jvp())/conv_general_dilated | solution.py:45
  56.5 0.9 slice_reduce_fusion.1
  57.4 1.3 copy.161
  58.7 1.0 reshape.305
  59.7 1.3 copy.153
  61.0 0.8 add_rsqrt_fusion
  61.9 1.4 multiply_reduce_fusion
  63.3 0.6 multiply_multiply_fusion.5
  64.1 1.0 reshape.301
  65.1 1.3 copy.162
  66.4 1.0 reshape.307
  67.4 1.3 copy.160
  68.7 1.0 reshape.303
  69.7 2.3 fusion.53
  73.1 9.6 %fusion.1 = f32[8,8,33,3]{1,3,2,0:T(4,128)S(1)} fusion(f32[8,8,33,3]{1,3,2,0:T(4,128)S(1)} %copy-done.27, f32[3,3,3,64]{3,2,1,0:T(4,128)S(1)} %copy-done.21, bf16[6,1,7,2,64]{4,2,3,0,1:T(8,128)(2,1)S(1)} %slice.125, bf16[6,1,8,33,64]{4,2,3,0,1:T(8,128)(2,1)S(1)} %copy.164, pred[8,33]{0,1:T(8,128)(4,1)S(1)} %copy-done.25), kind=kOutput, calls=%fused_computation.12 | convolution fusion | flops 6132096 | bytes 271368 | tf_op jit(solution)/shard_map/transpose(jvp())/conv_general_dilated | solution.py:45
  83.2 0.6 copy-done.1
  86.4 1.1 fusion.16
  87.5 1.1 fusion.21
  88.6 36.1 %all_to_all.10 = bf16[8,3,3,128,16]{3,4,2,1,0:T(8,128)(2,1)S(1)} all-to-all(bf16[8,3,3,128,16]{3,4,2,1,0:T(8,128)(2,1)S(1)} %copy.190), channel_id=1, replica_groups=mesh['dp'=8,'rows'=64] {'dp'}, dimensions={0} | all-to-all | bytes 589824 | tf_op jit(solution)/shard_map/all_to_all | solution.py:35
  124.7 0.7 convert_reduce_fusion
  125.9 0.6 copy.194
  126.6 4.0 %all-to-all-start.1 = ((bf16[8,16,3]{1,2,0:T(4,128)(2,1)}), bf16[8,16,3]{1,2,0:T(4,128)(2,1)S(1)}, u32[]{:S(2)}, u32[]{:S(2)}) async-start(bf16[8,16,3]{1,2,0:T(4,128)(2,1)} %copy.194), calls=%async_computation.1 | async-start | bytes 16384 | tf_op jit(solution)/shard_map/all_to_all | solution.py:35
  130.6 0.6 copy.195
  131.2 1.9 collective-permute-start.4
  133.1 2.4 collective-permute-start.5
  135.5 8.8 %all-to-all-done.1 = bf16[8,16,3]{1,2,0:T(4,128)(2,1)S(1)} async-done(((bf16[8,16,3]{1,2,0:T(4,128)(2,1)}), bf16[8,16,3]{1,2,0:T(4,128)(2,1)S(1)}, u32[]{:S(2)}, u32[]{:S(2)}) %all-to-all-start.1) | async-done | bytes 800 | tf_op jit(solution)/shard_map/all_to_all | solution.py:35
  144.3 121.4 %all-gather.2 = f32[64,16,3]{1,2,0:T(4,128)S(1)} all-gather(f32[1,16,3]{1,2,0:T(4,128)S(1)} %bitcast.392), channel_id=3, replica_groups=mesh['dp'=8,'rows'=64] {'rows'}, dimensions={0}, use_global_device_ids=true | all-gather | bytes 12480 | tf_op jit(solution)/shard_map/all_gather | solution.py:40
  265.8 0.7 reduce_sum.73
  266.8 0.8 fusion.4
  267.8 0.7 copy.196
  268.6 3.2 %reduce_sum.71 = f32[3,3,128,16]{2,3,1,0:T(8,128)} reduce(f32[64,3,3,128,16]{3,4,2,1,0:T(8,128)} %bitcast.373, f32[]{:T(128)} %constant.12.clone.1), dimensions={0}, to_apply=%region_4.5 | reduce | flops 1161216 | bytes 4792324 | tf_op jit(solution)/shard_map/reduce_sum | solution.py:41
  (132 shorter events, 12.4 us)
Async XLA Ops:
  7.2 25.7 %copy-start = (bf16[3,3,128,128]{3,2,1,0:T(8,128)(2,1)S(1)}, bf16[3,3,128,128]{3,2,1,0:T(8,128)(2,1)}, u32[]{:S(2)}) copy-start(bf16[3,3,128,128]{3,2,1,0:T(8,128)(2,1)} %param.9) | copy-start | bytes 884740
  7.2 19.3 %copy-start.22 = (pred[8,33]{0,1:T(8,128)(4,1)S(1)}, pred[8,33]{0,1:T(8,128)(4,1)}, u32[]{:S(2)}) copy-start(pred[8,33]{0,1:T(8,128)(4,1)} %constant.93) | copy-start | bytes 796
  7.2 18.6 %copy-start.8 = (f32[1,4,256,3]{2,1,3,0:T(4,128)S(1)}, f32[1,4,256,3]{2,1,3,0:T(4,128)}, u32[]{:S(2)}) copy-start(f32[1,4,256,3]{2,1,3,0:T(4,128)} %param.11) | copy-start | bytes 36868
  7.2 19.2 %copy-start.19 = (f32[3,3,3,64]{3,2,1,0:T(4,128)S(1)}, f32[3,3,3,64]{3,2,1,0:T(4,128)}, u32[]{:S(2)}) copy-start(f32[3,3,3,64]{3,2,1,0:T(4,128)} %param.14) | copy-start | bytes 20740
  7.2 261.4 %all-gather.5.cloned.1.call-start = ((), (), s32[]{:S(2)}) async-start(), calls=%async_computation.2 | async-start | bytes 4792320 | tf_op jit(solution)/shard_map/all_gather | solution.py:40
  8.0 17.8 %collective-permute-start.2 = (bf16[1,2,256,3]{2,1,3,0:T(2,128)(2,1)S(1)}, bf16[1,2,256,3]{2,1,3,0:T(2,128)(2,1)S(1)}, u32[]{:S(2)}, u32[]{:S(2)}) collective-permute-start(bf16[1,2,256,3]{2,1,3,0:T(2,128)(2,1)S(1)} %get-tuple-element.35), channel_id=1, source_target_pairs={{0,1},{1,2},{2,3},{3,4},{4,5},{5,6},{6,7},{7,8},{8,9},{9,10},{10,1... | collective-permute-start | bytes 9224 | tf_op jit(solution)/shard_map/ppermute | solution.py:18
  12.5 13.3 %collective-permute-start.3 = (bf16[1,2,256,3]{2,1,3,0:T(2,128)(2,1)S(1)}, bf16[1,2,256,3]{2,1,3,0:T(2,128)(2,1)S(1)}, u32[]{:S(2)}, u32[]{:S(2)}) collective-permute-start(bf16[1,2,256,3]{2,1,3,0:T(2,128)(2,1)S(1)} %get-tuple-element.36), channel_id=1, source_target_pairs={{1,0},{2,1},{3,2},{4,3},{5,4},{6,5},{7,6},{8,7},{9,8},{10,9},{11,1... | collective-permute-start | bytes 9224 | tf_op jit(solution)/shard_map/ppermute | solution.py:20
  19.2 11.6 %collective-permute-start = (bf16[1,3,256,128]{2,3,1,0:T(8,128)(2,1)S(1)}, bf16[1,3,256,128]{2,3,1,0:T(8,128)(2,1)}, u32[]{:S(2)}, u32[]{:S(2)}) collective-permute-start(bf16[1,3,256,128]{2,3,1,0:T(8,128)(2,1)S(1)} %get-tuple-element.31), channel_id=1, source_target_pairs={{0,1},{1,2},{2,3},{3,4},{4,5},{5,6},{6,7},{7,8},{8,9},{9,10},{10,1... | collective-permute-start | bytes 589832 | tf_op jit(solution)/shard_map/ppermute | solution.py:18
  21.1 9.7 %collective-permute-start.1 = (bf16[1,3,256,128]{2,3,1,0:T(8,128)(2,1)S(1)}, bf16[1,3,256,128]{2,3,1,0:T(8,128)(2,1)}, u32[]{:S(2)}, u32[]{:S(2)}) collective-permute-start(bf16[1,3,256,128]{2,3,1,0:T(8,128)(2,1)S(1)} %get-tuple-element.32), channel_id=1, source_target_pairs={{1,0},{2,1},{3,2},{4,3},{5,4},{6,5},{7,6},{8,7},{9,8},{10,9},{11,1... | collective-permute-start | bytes 589832 | tf_op jit(solution)/shard_map/ppermute | solution.py:20
  32.7 0.7 copy-start.23
  35.0 1.2 copy-start.3
  36.2 0.7 copy-start.15
  36.2 0.7 copy-start.26
  36.2 1.1 copy-start.9
  38.2 1.1 copy-start.20
  39.3 3.3 %copy-start.17 = (f32[3,3,3,64]{3,2,1,0:T(4,128)S(1)}, f32[3,3,3,64]{3,2,1,0:T(4,128)}, u32[]{:S(2)}) copy-start(f32[3,3,3,64]{3,2,1,0:T(4,128)} %param.12) | copy-start | bytes 20740
  45.0 0.7 copy-start.18
  45.0 0.7 copy-start.24
  45.7 10.6 %copy-start.7 = (f32[6,8,33,64]{3,1,2,0:T(8,128)S(1)}, f32[6,8,33,64]{3,1,2,0:T(8,128)}, u32[]{:S(2)}) copy-start(f32[6,8,33,64]{3,1,2,0:T(8,128)} %get-tuple-element.22) | copy-start | bytes 1216516
  61.0 2.3 copy-start.12
  61.0 2.9 %copy-start.6 = (f32[6,8,33,64]{3,1,2,0:T(8,128)S(1)}, f32[6,8,33,64]{3,1,2,0:T(8,128)}, u32[]{:S(2)}) copy-start(f32[6,8,33,64]{3,1,2,0:T(8,128)} %get-tuple-element.25) | copy-start | bytes 1216516
  61.8 2.1 copy-start.10
  61.9 2.1 copy-start.11
  72.0 0.7 copy-start.21
  72.0 0.7 copy-start.25
  72.0 1.1 copy-start.27
  73.1 10.0 %copy-start.2 = (f32[4,1,256,128]{3,0,2,1:T(4,128)S(1)}, f32[4,1,256,128]{3,0,2,1:T(4,128)}, u32[]{:S(2)}) copy-start(f32[4,1,256,128]{3,0,2,1:T(4,128)} %slice.132) | copy-start | bytes 1572868
  73.1 10.0 %copy-start.13 = (f32[1,4,256,3]{2,3,1,0:T(4,128)S(1)}, f32[1,4,256,3]{2,3,1,0:T(4,128)}, u32[]{:S(2)}) copy-start(f32[1,4,256,3]{2,3,1,0:T(4,128)} %get-tuple-element.33) | copy-start | bytes 36868
  73.1 10.0 %copy-start.16 = (bf16[128,3]{0,1:T(4,128)(2,1)S(1)}, bf16[128,3]{0,1:T(4,128)(2,1)}, u32[]{:S(2)}) copy-start(bf16[128,3]{0,1:T(4,128)(2,1)} %param.10) | copy-start | bytes 2308
  82.7 1.1 copy-start.1
  82.7 1.4 copy-start.5
  88.5 36.9 %copy-start.4 = (bf16[8,8,33,128]{3,1,2,0:T(8,128)(2,1)S(1)}, bf16[8,8,33,128]{3,1,2,0:T(8,128)(2,1)}, u32[]{:S(2)}) copy-start(bf16[8,8,33,128]{3,1,2,0:T(8,128)(2,1)} %copy-done.3) | copy-start | bytes 1622020
  125.4 5.1 %copy-start.14 = (f32[1,4,256,3]{2,3,1,0:T(4,128)S(1)}, f32[1,4,256,3]{2,3,1,0:T(4,128)}, u32[]{:S(2)}) copy-start(f32[1,4,256,3]{2,3,1,0:T(4,128)} %get-tuple-element.34) | copy-start | bytes 36868
  126.6 17.8 %all-to-all-start.1 = ((bf16[8,16,3]{1,2,0:T(4,128)(2,1)}), bf16[8,16,3]{1,2,0:T(4,128)(2,1)S(1)}, u32[]{:S(2)}, u32[]{:S(2)}) async-start(bf16[8,16,3]{1,2,0:T(4,128)(2,1)} %copy.194), calls=%async_computation.1 | async-start | bytes 16384 | tf_op jit(solution)/shard_map/all_to_all | solution.py:35
  131.2 135.2 %collective-permute-start.4 = (bf16[1,1,256,128]{3,2,1,0:T(8,128)(2,1)S(1)}, bf16[1,1,256,128]{3,2,1,0:T(8,128)(2,1)S(1)}, u32[]{:S(2)}, u32[]{:S(2)}) collective-permute-start(bf16[1,1,256,128]{3,2,1,0:T(8,128)(2,1)S(1)} %get-tuple-element.29), channel_id=1, source_target_pairs={{0,1},{1,2},{2,3},{3,4},{4,5},{5,6},{6,7},{7,8},{8,9},{9,10},{10,1... | collective-permute-start | bytes 196616 | tf_op jit(solution)/shard_map/ppermute | solution.py:18
  133.1 133.3 %collective-permute-start.5 = (bf16[1,1,256,128]{3,2,1,0:T(8,128)(2,1)S(1)}, bf16[1,1,256,128]{3,2,1,0:T(8,128)(2,1)S(1)}, u32[]{:S(2)}, u32[]{:S(2)}) collective-permute-start(bf16[1,1,256,128]{3,2,1,0:T(8,128)(2,1)S(1)} %get-tuple-element.30), channel_id=1, source_target_pairs={{1,0},{2,1},{3,2},{4,3},{5,4},{6,5},{7,6},{8,7},{9,8},{10,9},{11,1... | collective-permute-start | bytes 196616 | tf_op jit(solution)/shard_map/ppermute | solution.py:20
Sparse Core Ops, SparseCore 0:
  125.6 120.5 all-gather.4
where the time goes:
time: 280 us; the launch traced here: 279 us
  blocking collectives  158 us (56%)
  matrix products  34 us (12%)
  local copies, waits for them, and re-layouts  24.2 us (9%)
  starting transfers between devices  23.4 us (8%)
  other arithmetic  15.9 us (6%)
  between operations  14.8 us (5%)
  waiting for transfers between devices  8.83 us (3%)
    all_gather x1, blocking collectives, over_pieces(): tiles = lax.all_gather(array, axis)  121 us
    all_to_all x1, blocking collectives, sent_and_summed(): lax.all_to_all(tiles, axis, split_axis=0, concat_axis=0, tiled=True)  36.1 us
    conv_general_dilated x7, matrix products, convolve(): lax.conv_general_dilated(inputs, kernel, (1, 1), padding, dimension_numbe...  29.1 us
    ppermute x3, starting transfers between devices, padded_2(): lax.ppermute(head, axis, [((i + 1) % count, i) for i in range(ends)])  11 us
    all_to_all x1, waiting for transfers between devices, sent_and_summed(): lax.all_to_all(tiles, axis, split_axis=0, concat_axis=0, tiled=True)  8.8 us
    ppermute x3, starting transfers between devices, padded_2(): lax.ppermute(tail, axis, [(i, (i + 1) % count) for i in range(ends)])  8.32 us
    mul x8, local copies, waits for them, and re-layouts, tile_loss(): jax.nn.gelu(convolve(images, lpips_weight, side, high), approximate=True)  7.07 us
    unnamed x60, local copies, waits for them, and re-layouts  5.99 us
  transfers between devices with their start and end apart: 8, of which 1 were waited for; matrix products, arithmetic and copies ran while one was open for 4% of the time, Pallas kernels for 0%

commit v1 on v0

v1 whole, which is shorter than its diff:
```python
import functools

import jax
import jax.numpy as jnp
import numpy as np
from jax import lax
from jax.experimental import pallas as pl
from jax.experimental.pallas import tpu as pltpu
from jax.sharding import Mesh, PartitionSpec as P

ADV_SCALE = 0.5
CHARB_EPS = 0.01
NORM_EPS = 1e-06
GELU_K = 0.7978845608028654
GELU_C = 0.044715

ROWS_LOC = 4
COLS = 256
CH = 128
TILES = 64
HEIGHT = ROWS_LOC * TILES
N_PRE = 10
N_LOSS = 8
N_GRAD = 6
PITCH = COLS + 8
K_BAND = 256
BLOCK = 20
PADDED = 24
VMEM = pltpu.VMEM


def band_selectors():
    ahead = np.zeros((32, N_LOSS * K_BAND), np.float32)
    back = np.zeros((N_LOSS * 3 * N_GRAD * 8, 32), np.float32)
    for a in range(3):
        for b in range(3):
            for c in range(3):
                tap = (a * 3 + b) * 3 + c
                for r in range(N_LOSS):
                    ahead[tap, r * K_BAND + b * N_PRE * 8 + (r + a) * 8 + c] = 1.0
                    q = r + a - 2
                    if 0 <= q < N_GRAD:
                        back[r * 3 * N_GRAD * 8 + b * N_GRAD * 8 + q * 8 + c, tap] = 1.0
    return ahead, back


def dot(a, b, ca, cb):
    return lax.dot_general(a, b, (((ca,), (cb,)), ((), ())), preferred_element_type=jnp.float32)


def sigmoid(x):
    return 0.5 * jnp.tanh(0.5 * x) + 0.5


def shifted(x, by):
    lane = lax.broadcasted_iota(jnp.int32, x.shape, 1)
    if by == 1:
        return jnp.where(lane == 0, 0.0, pltpu.roll(x, 1, 1))
    return jnp.where(lane == COLS - 1, 0.0, pltpu.roll(x, COLS - 1, 1))


def prep_kernel(w27_ref, ahead_ref, back_ref, band_ref, band_t_ref):
    w27 = w27_ref[...].astype(jnp.bfloat16)
    size = 3 * N_GRAD * 8
    for r in range(N_LOSS):
        band = dot(w27, ahead_ref[:, r * K_BAND : (r + 1) * K_BAND], 0, 0)
        band_ref[r * CH : (r + 1) * CH, :] = band.astype(jnp.bfloat16)
        back = dot(back_ref[r * size : (r + 1) * size, :], w27, 1, 0)
        band_t_ref[:, r * CH : (r + 1) * CH] = back.astype(jnp.bfloat16)


def main_kernel(
    tile_ref, up_ref, own_ref, down_ref, t_up_ref, t_own_ref, t_down_ref, conv_ref, out_w_ref,
    band_ref, band_t_ref, heads_ref,
    recon_ref, grad_pre_ref, piece_ref,
    y0, y1, y2, slope, hidden, truth, dall, packed,
):
    bf16, f32 = jnp.bfloat16, jnp.float32
    first_row = tile_ref[0] * ROWS_LOC

    def valid(row):
        inside = jnp.logical_and(first_row + row >= 0, first_row + row < HEIGHT)
        return jnp.where(inside, 1.0, 0.0).astype(f32)

    def feats(j):
        return (up_ref, own_ref, down_ref)[j // ROWS_LOC][j % ROWS_LOC]

    for buf in (y0, y2):
        for j in range(N_PRE + 1):
            buf[pl.ds(j * PITCH, 8), :] = jnp.zeros((8, CH), f32)
    weights = jnp.concatenate(
        [jnp.concatenate([conv_ref[a, b] for a in range(3)], axis=0) for b in range(3)], axis=1
    )
    out_w = out_w_ref[...]
    out_w16 = out_w.astype(bf16)
    image = []
    for j in range(N_PRE):
        lhs = jnp.concatenate([feats(j), feats(j + 1), feats(j + 2)], axis=1)
        prod = dot(lhs, weights, 1, 0)
        for b, buf in enumerate((y0, y1, y2)):
            buf[pl.ds(j * PITCH + 8, COLS), :] = prod[:, b * CH : (b + 1) * CH]
    for j in range(N_PRE):
        at = j * PITCH + 8
        pre = y0[pl.ds(at - 1, COLS), :] + y1[pl.ds(at, COLS), :] + y2[pl.ds(at + 1, COLS), :]
        sig = sigmoid(pre)
        act = (pre * sig).astype(bf16)
        if 2 <= j < 2 + N_GRAD:
            slope[j - 2] = sig * (1.0 + pre * (1.0 - sig))
        if 3 <= j < 3 + ROWS_LOC:
            hidden[j - 3] = act
        image.append(dot(out_w16, act, 1, 1) * valid(j - 3))
    for j in range(ROWS_LOC):
        for c in range(3):
            recon_ref[c, j : j + 1, :] = image[j + 3][c : c + 1, :]
    image = jnp.concatenate(image, axis=0)

    truth[...] = jnp.zeros_like(truth)
    for j in range(N_PRE):
        k = j + 1
        src = (t_up_ref, t_own_ref, t_down_ref)[k // ROWS_LOC]
        for c in range(3):
            truth[j * 8 + c : j * 8 + c + 1, :] = src[c, k % ROWS_LOC : k % ROWS_LOC + 1, :]
    true_image = truth[...]

    def taps(x):
        pad = jnp.zeros((K_BAND - 3 * N_PRE * 8, COLS), f32)
        return jnp.concatenate([shifted(x, 1), x, shifted(x, -1), pad], axis=0).astype(bf16)

    taps_a, taps_b = taps(image), taps(true_image)
    half = CH // 2

    def gelu(x):
        sq = x * x
        th = jnp.tanh(GELU_K * x * (1.0 + GELU_C * sq))
        low = 0.5 * (1.0 + th)
        return x * low, low, th, sq

    for r in range(N_LOSS):
        ok = valid(r - 2)
        both = dot(band_ref[r * CH : (r + 1) * CH, :], taps_a, 1, 0)
        other = dot(band_ref[r * CH + half : (r + 1) * CH, :], taps_b, 1, 0)
        for side in range(2):
            cols = slice(side * CH, (side + 1) * CH)
            g, a, t = both[:half, cols], both[half:, cols], other[:, cols]
            d_disc = (heads_ref[:half, :] * ok) * (0.2 + 0.8 * sigmoid(g))
            fa, low, th, sq = gelu(a)
            fb = gelu(t)[0]
            inv_a = lax.rsqrt(jnp.sum(fa * fa, axis=0, keepdims=True) * (1.0 / half) + NORM_EPS)
            inv_b = lax.rsqrt(jnp.sum(fb * fb, axis=0, keepdims=True) * (1.0 / half) + NORM_EPS)
            na = fa * inv_a
            up = (heads_ref[half:, :] * ok) * (na - fb * inv_b)
            mean = jnp.sum(up * na, axis=0, keepdims=True) * (1.0 / half)
            d_feat = inv_a * (up - na * mean)
            rise = low + 0.5 * a * (1.0 - th * th) * (GELU_K * (1.0 + 3.0 * GELU_C * sq))
            dall[r * CH : r * CH + half, cols] = d_disc.astype(bf16)
            dall[r * CH + half : (r + 1) * CH, cols] = (d_feat * rise).astype(bf16)

    back = dot(band_t_ref[...], dall[...], 1, 0)
    n = N_GRAD * 8
    diff = (image - true_image)[16 : 16 + n]
    grad_image = (
        shifted(back[:n], -1) + back[n : 2 * n] + shifted(back[2 * n :], 1)
        + diff * lax.rsqrt(diff * diff + CHARB_EPS)
    )
    out_w2 = jnp.concatenate([out_w, out_w], axis=0).astype(bf16)
    grad_out = jnp.zeros((16, CH), f32)
    for q in range(N_GRAD):
        g = grad_image[q * 8 : (q + 1) * 8] * valid(q - 1)
        high = g.astype(bf16).astype(f32)
        pair = jnp.concatenate([high, g - high], axis=0)
        grad_pre = dot(pair.T.astype(bf16), out_w2, 1, 0) * slope[q]
        grad_pre_ref[q] = grad_pre.astype(bf16)
        if 1 <= q <= ROWS_LOC:
            y0[pl.ds((q - 1) * PITCH + 8, COLS), :] = grad_pre
            grad_out = grad_out + dot(pair.astype(bf16), hidden[q - 1], 1, 0)
    grad_out = grad_out[:8] + grad_out[8:]

    lhs, rhs = [], []
    for y in range(ROWS_LOC):
        at = y * PITCH + 8
        lhs.append(
            jnp.concatenate([y0[pl.ds(at + 1 - b, COLS), :] for b in range(3)], axis=1).astype(bf16)
        )
        rhs.append(jnp.concatenate([feats(3 + y + a) for a in range(3)], axis=1))
    lhs, rhs = jnp.concatenate(lhs, axis=0), jnp.concatenate(rhs, axis=0)
    packed[...] = jnp.zeros_like(packed)
    for b in range(3):
        grad = dot(lhs[:, b * CH : (b + 1) * CH], rhs, 0, 0)
        for a in range(3):
            tap = a * 3 + b
            for d in range(8):
                block = grad[d * 16 : (d + 1) * 16, a * CH : (a + 1) * CH]
                start = tap * 16
                while start < tap * 16 + 16:
                    part, inner = divmod(start, 18)
                    count = min(18 - inner, tap * 16 + 16 - start)
                    at = ((d // 2) * 8 + part) * 2 * BLOCK + (d % 2) * BLOCK + inner
                    packed[pl.ds(at, count), :] = block[start - tap * 16 : start - tap * 16 + count]
                    start += count
    for d in range(8):
        for c in range(3):
            line = grad_out[c : c + 1]
            if d:
                line = pltpu.roll(line, CH - 16 * d, 1)
            packed[pl.ds(((d // 2) * 8 + c) * 2 * BLOCK + (d % 2) * BLOCK + 18, 1), :] = line
    piece_ref[...] = packed[...].astype(bf16)


def back_kernel(grad_ref, conv_ref, out_ref, z0, z1, z2):
    bf16, f32 = jnp.bfloat16, jnp.float32
    for buf in (z0, z2):
        for y in range(ROWS_LOC + 1):
            buf[pl.ds(y * PITCH, 8), :] = jnp.zeros((8, CH), f32)
    weights = jnp.concatenate(
        [jnp.concatenate([conv_ref[a, b] for a in range(3)], axis=1) for b in range(3)], axis=0
    )
    for y in range(ROWS_LOC):
        lhs = jnp.concatenate([grad_ref[y + 2 - a] for a in range(3)], axis=1)
        prod = dot(lhs, weights, 1, 1)
        for b, buf in enumerate((z0, z1, z2)):
            buf[pl.ds(y * PITCH + 8, COLS), :] = prod[:, b * CH : (b + 1) * CH]
    for y in range(ROWS_LOC):
        at = y * PITCH + 8
        total = z0[pl.ds(at + 1, COLS), :] + z1[pl.ds(at, COLS), :] + z2[pl.ds(at - 1, COLS), :]
        out_ref[y] = total.astype(bf16)


def first_sum_kernel(in_ref, out_ref):
    total = in_ref[0].astype(jnp.float32)
    for k in range(1, in_ref.shape[0]):
        total = total + in_ref[k].astype(jnp.float32)
    pad = jnp.zeros((PADDED - BLOCK, CH), jnp.float32)
    for half in range(2):
        part = jnp.concatenate([total[half * BLOCK : (half + 1) * BLOCK], pad], axis=0)
        for k in range(8):
            out_ref[half * 8 + k] = part.astype(jnp.bfloat16)


def second_sum_kernel(in_ref, out_ref):
    total = in_ref[0].astype(jnp.float32)
    for k in range(1, in_ref.shape[0]):
        total = total + in_ref[k].astype(jnp.float32)
    for k in range(8):
        out_ref[k] = total


def last_kernel(in_ref, conv_ref, out_ref):
    for k in range(8):
        conv_ref[pl.ds(k * 18, 18), :] = in_ref[k, 0:18, :]
    for c in range(3):
        out_ref[c : c + 1, :] = in_ref[c, 18:19, :16]


def call(kernel, out_shape, scratch=(), smem=0, n_in=1, flops=0, name=None):
    specs = [pl.BlockSpec(memory_space=pltpu.SMEM)] * smem
    specs += [pl.BlockSpec(memory_space=VMEM)] * (n_in - smem)
    many = isinstance(out_shape, tuple)
    return pl.pallas_call(
        kernel,
        out_shape=out_shape,
        in_specs=specs,
        out_specs=tuple(pl.BlockSpec(memory_space=VMEM) for _ in out_shape)
        if many
        else pl.BlockSpec(memory_space=VMEM),
        scratch_shapes=list(scratch),
        cost_estimate=pl.CostEstimate(flops=flops, bytes_accessed=1 << 20, transcendentals=0),
        name=name,
    )


def shape(*dims, dtype=jnp.float32):
    return jax.ShapeDtypeStruct(dims, dtype)


def prepare(disc_weight, disc_head, lpips_weight, lpips_lin, out_weight):
    f32 = jnp.float32
    ahead, back = band_selectors()
    w27 = jnp.concatenate([disc_weight.reshape(27, 64), lpips_weight.reshape(27, 64)], axis=1)
    w27 = jnp.pad(w27, ((0, 5), (0, 0)))
    heads = jnp.concatenate([-ADV_SCALE * disc_head, 2.0 * lpips_lin])
    heads = jnp.broadcast_to(heads[:, None], (128, 128))
    out_w = jnp.pad(out_weight.astype(f32).T, ((0, 5), (0, 0)))
    band, band_t = call(
        prep_kernel,
        (
            shape(N_LOSS * CH, K_BAND, dtype=jnp.bfloat16),
            shape(3 * N_GRAD * 8, N_LOSS * CH, dtype=jnp.bfloat16),
        ),
        n_in=3,
        flops=1 << 28,
        name="bands",
    )(w27, jnp.asarray(ahead, jnp.bfloat16), jnp.asarray(back, jnp.bfloat16))
    return band, band_t, heads, out_w


def tile_step(tile, up, own, down, t_up, t_own, t_down, conv_weight, out_w, band, band_t, heads):
    f32, bf16 = jnp.float32, jnp.bfloat16
    rows = N_PRE * PITCH + 8
    return call(
        main_kernel,
        (
            shape(3, ROWS_LOC, COLS),
            shape(N_GRAD, COLS, CH, dtype=bf16),
            shape(32 * 2 * BLOCK, CH, dtype=bf16),
        ),
        scratch=[
            VMEM((rows, CH), f32),
            VMEM((rows, CH), f32),
            VMEM((rows, CH), f32),
            VMEM((N_GRAD, COLS, CH), f32),
            VMEM((ROWS_LOC, COLS, CH), bf16),
            VMEM((N_PRE * 8, COLS), f32),
            VMEM((N_LOSS * CH, COLS), bf16),
            VMEM((32 * 2 * BLOCK, CH), f32),
        ],
        smem=1,
        n_in=12,
        flops=1 << 31,
        name="tile",
    )(tile, up, own, down, t_up, t_own, t_down, conv_weight, out_w, band, band_t, heads)


def back_step(grad_pre, conv_weight):
    rows = ROWS_LOC * PITCH + 8
    return call(
        back_kernel,
        shape(ROWS_LOC, COLS, CH, dtype=jnp.bfloat16),
        scratch=[VMEM((rows, CH), jnp.float32)] * 3,
        n_in=2,
        flops=1 << 30,
        name="features_back",
    )(grad_pre, conv_weight)


def swap(array, axes):
    return lax.all_to_all(array, axes, split_axis=0, concat_axis=0, tiled=True)


ROWS = ("zl", "x", "core")


def body(
    features, conv_weight, out_weight, targets, disc_weight, disc_head, lpips_weight, lpips_lin
):
    own = features[0]
    t_own = jnp.transpose(targets[0], (2, 0, 1))
    fall = [(i, i + 1) for i in range(TILES - 1)]
    rise = [(i + 1, i) for i in range(TILES - 1)]
    up, down = lax.ppermute(own, ROWS, fall), lax.ppermute(own, ROWS, rise)
    t_up, t_down = lax.ppermute(t_own, ROWS, fall), lax.ppermute(t_own, ROWS, rise)
    band, band_t, heads, out_w = prepare(
        disc_weight, disc_head, lpips_weight, lpips_lin, out_weight
    )
    tile = lax.axis_index(ROWS).astype(jnp.int32).reshape(1)
    recon, grad_pre, pieces = tile_step(
        tile, up, own, down, t_up, t_own, t_down, conv_weight, out_w, band, band_t, heads
    )
    grad_features = back_step(grad_pre, conv_weight)
    pieces = swap(pieces.reshape(32, 2 * BLOCK, CH), ("y", "x", "core"))
    pieces = call(first_sum_kernel, shape(16, PADDED, CH, dtype=jnp.bfloat16), name="sum_1")(pieces)
    pieces = swap(pieces, ("zh", "zl"))
    pieces = call(second_sum_kernel, shape(8, PADDED, CH), name="sum_2")(pieces)
    pieces = swap(pieces, ("x", "core"))
    grad_conv, grad_out = call(last_kernel, (shape(144, CH), shape(3, 16)), name="join")(pieces)
    return (
        jnp.transpose(recon, (1, 2, 0))[None],
        grad_features[None],
        jnp.transpose(grad_conv.reshape(3, 3, 16, CH), (0, 1, 3, 2)),
        grad_out.T,
    )


def solution(mesh):
    fine = Mesh(mesh.devices.reshape(4, 2, 8, 4, 2), ("y", "zh", "zl", "x", "core"))
    dp = ("y", "zh")
    in_specs = (
        P(dp, ROWS, None, None), P(), P(), P(dp, ROWS, None, None), P(), P(), P(), P(),
    )
    out_specs = (
        P(dp, ROWS, None, None), P(dp, ROWS, None, None), P(None, None, None, dp), P(dp, None),
    )
    return jax.shard_map(body, mesh=fine, in_specs=in_specs, out_specs=out_specs, check_vma=False)
```

time: 280 us -> 90.9 us (0.32)
  blocking collectives: 158 us -> 44.5 us
  matrix products: 34 us -> 0 us
  local copies, waits for them, and re-layouts: 24.2 us -> 2.86 us
  Pallas kernels: 0 us -> 16.1 us
  other arithmetic: 15.9 us -> 1.35 us
  between operations: 14.8 us -> 0.78 us
  waiting for transfers between devices: 8.83 us -> 2.45 us
    all_gather x1 -> x0, blocking collectives: 121 us -> none  [over_pieces(): tiles = lax.all_gather(array, axis)]
    conv_general_dilated x7 -> x0, matrix products: 29.1 us -> none  [convolve(): lax.conv_general_dilated(inputs, kernel, (1, 1), padding, dimension_numbe...]
    pallas_call x0 -> x6, Pallas kernels: none -> 16.1 us  [the longest x1 6.43 us: tile_step(): call(main_kernel, (shape(3, ROWS_LOC, COLS), shape(N_GRAD, COLS, CH, dtyp...]
    mul x15 -> x0, local copies, waits for them, and re-layouts: 8.99 us -> none  [the longest x8 7.07 us: tile_loss(): jax.nn.gelu(convolve(images, lpips_weight, side, high), approximate=True)]
    all_to_all x1 -> x2, blocking collectives: 36.1 us -> 44.5 us  [swap(): return lax.all_to_all(array, axes, split_axis=0, concat_axis=0, tiled=True)]
    reduce_sum x7 -> x0, other arithmetic: 7.78 us -> none  [the longest x2 3.9 us: over_pieces(): return tiles.sum(axis=0)]
    all_to_all x1, waiting for transfers between devices: 8.8 us -> 2.44 us  [swap(): return lax.all_to_all(array, axes, split_axis=0, concat_axis=0, tiled=True)]
    dot_general x12 -> x0, matrix products: 4.88 us -> none  [the longest x9 4.21 us: weight_taps(): lax.dot_general(window, flat_grad, (((0,), (0,)), ((), ())), preferred_el...]
  transfers between devices with their start and end apart: 8 -> 5, of which waited for: 1 -> 1; matrix products, arithmetic and copies ran while one was open for 4% -> 2% of each run, Pallas kernels for 0% -> 5%
where the time goes in v1:
time: 90.9 us; the launch traced here: 90.2 us
  blocking collectives  44.5 us (49%)
  starting transfers between devices  22.2 us (24%)
  Pallas kernels  16.1 us (18%)
  local copies, waits for them, and re-layouts  2.86 us (3%)
  waiting for transfers between devices  2.45 us (3%)
  other arithmetic  1.35 us (1%)
    all_to_all x2, blocking collectives, swap(): return lax.all_to_all(array, axes, split_axis=0, concat_axis=0, tiled=True)  44.5 us
    ppermute x1, starting transfers between devices, body(): lax.ppermute(t_own, ROWS, rise)  8.88 us
    pallas_call x1, Pallas kernels, tile_step(): call(main_kernel, (shape(3, ROWS_LOC, COLS), shape(N_GRAD, COLS, CH, dtyp...  6.43 us
    all_to_all x1, starting transfers between devices, swap(): return lax.all_to_all(array, axes, split_axis=0, concat_axis=0, tiled=True)  5.79 us
    ppermute x2, starting transfers between devices, body(): up, down = (lax.ppermute(own, ROWS, fall), lax.ppermute(own, ROWS, rise))  5.57 us
    pallas_call x1, Pallas kernels, back_step(): call(back_kernel, shape(ROWS_LOC, COLS, CH, dtype=jnp.bfloat16), scratch=...  2.56 us
    all_to_all x1, waiting for transfers between devices, swap(): return lax.all_to_all(array, axes, split_axis=0, concat_axis=0, tiled=True)  2.44 us
    pallas_call x1, Pallas kernels, prepare(): call(prep_kernel, (shape(N_LOSS * CH, K_BAND, dtype=jnp.bfloat16), shape(...  2.37 us
  transfers between devices with their start and end apart: 5, of which 1 were waited for; matrix products, arithmetic and copies ran while one was open for 2% of the time, Pallas kernels for 5%

profile of v1, /device:TPU:1, one launch (start us, length us, event | category | flops | bytes accessed | tf_op | source)
XLA Modules:
  0.0 90.2 jit_solution(10348701175966740469)
XLA Ops:
  0.6 0.0 copy-start.3
  0.6 0.0 copy-start.4
  0.7 8.9 %collective-permute-start.3 = (f32[3,4,256]{2,1,0:T(4,128)}, f32[3,4,256]{2,1,0:T(4,128)S(1)}, u32[]{:S(2)}, u32[]{:S(2)}) collective-permute-start(f32[3,4,256]{2,1,0:T(4,128)} %bitcast.21), channel_id=1, source_target_pairs={{1,0},{2,1},{3,2},{4,3},{5,4},{6,5},{7,6},{8,7},{9,8},{10,9},{11,1... | collective-permute-start | bytes 36872 | tf_op jit(solution)/shard_map/ppermute | solution.py:350
  9.5 1.9 %collective-permute-start.2 = (f32[3,4,256]{2,1,0:T(4,128)}, f32[3,4,256]{2,1,0:T(4,128)S(1)}, u32[]{:S(2)}, u32[]{:S(2)}) collective-permute-start(f32[3,4,256]{2,1,0:T(4,128)} %bitcast.22), channel_id=1, source_target_pairs={{0,1},{1,2},{2,3},{3,4},{4,5},{5,6},{6,7},{7,8},{8,9},{9,10},{10,1... | collective-permute-start | bytes 36872 | tf_op jit(solution)/shard_map/ppermute | solution.py:350
  11.5 2.4 %collective-permute-start.1 = (bf16[4,256,128]{2,1,0:T(8,128)(2,1)}, bf16[4,256,128]{2,1,0:T(8,128)(2,1)S(1)}, u32[]{:S(2)}, u32[]{:S(2)}) collective-permute-start(bf16[4,256,128]{2,1,0:T(8,128)(2,1)} %bitcast.17), channel_id=1, source_target_pairs={{1,0},{2,1},{3,2},{4,3},{5,4},{6,5},{7,6},{8,7},{9,8},{10,9},{11,1... | collective-permute-start | bytes 786440 | tf_op jit(solution)/shard_map/ppermute | solution.py:349
  13.9 3.2 %collective-permute-start = (bf16[4,256,128]{2,1,0:T(8,128)(2,1)}, bf16[4,256,128]{2,1,0:T(8,128)(2,1)S(1)}, u32[]{:S(2)}, u32[]{:S(2)}) collective-permute-start(bf16[4,256,128]{2,1,0:T(8,128)(2,1)} %bitcast.18), channel_id=1, source_target_pairs={{0,1},{1,2},{2,3},{3,4},{4,5},{5,6},{6,7},{7,8},{8,9},{9,10},{10,1... | collective-permute-start | bytes 786440 | tf_op jit(solution)/shard_map/ppermute | solution.py:349
  17.1 0.0 copy-done.3
  17.1 0.0 copy-done.4
  17.1 0.0 copy-start.1
  17.1 0.1 pad_maximum_fusion
  17.2 0.7 reshape.25
  17.9 0.0 copy-done.1
  17.9 0.0 copy-start.2
  17.9 0.7 copy-done.2
  18.6 0.6 pad_convert_fusion.out_w_ref
  19.2 0.7 select_maximum_fusion.w27_ref
  19.9 2.4 %bands.1 = (bf16[1024,256]{1,0:T(8,128)(2,1)}, bf16[144,1024]{1,0:T(8,128)(2,1)}) custom-call(f32[32,128]{1,0:T(8,128)} %select_maximum_fusion.w27_ref, bf16[32,2048]{1,0:T(8,128)(2,1)} %constant.29.clone.ahead_ref, bf16[1152,32]{1,0:T(8,128)(2,1)} %constant.30.clone.back_ref), custom_call_target="tpu_custom_call" | custom-call | flops 268435456 | bytes 1048576 | tf_op jit(solution)/shard_map/bands/pallas_call | solution.py:283
  22.3 0.0 collective-permute-done.3.t_down_ref
  22.3 0.0 copy-start.7
  22.3 0.0 collective-permute-done.2.t_up_ref
  22.3 0.0 copy-start.8
  22.3 0.0 collective-permute-done.1.down_ref
  22.3 0.0 copy-start.5
  22.3 0.0 collective-permute-done.up_ref
  22.3 0.0 copy-start.6
  22.3 0.8 broadcast_in_dim.12.heads_ref
  23.1 0.0 copy-done.7
  23.1 0.0 copy-done.8
  23.1 0.0 copy-done.5
  23.1 0.0 copy-done.6
  23.1 6.4 %tile.1 = (f32[3,4,256]{2,1,0:T(4,128)}, bf16[6,256,128]{2,1,0:T(8,128)(2,1)}, bf16[1280,128]{1,0:T(8,128)(2,1)}) custom-call(s32[1]{0:T(128)} %bitcast.tile_ref, bf16[4,256,128]{2,1,0:T(8,128)(2,1)} %copy-done.6, bf16[4,256,128]{2,1,0:T(8,128)(2,1)} %bitcast.19, bf16[4,256,128]{2,1,0:T(8,128)(2,1)} %copy-done.5, f32[3,4,256]{2,1,0:T(4,128)} %copy-done.8, ...), custom_call_target="tpu_custom_call" | custom-call | flops 2147483648 | bytes 1048576 | tf_op jit(solution)/shard_map/tile/pallas_call | solution.py:299
  29.5 16.5 %all_to_all.15.in_ref = bf16[32,40,128]{2,1,0:T(8,128)(2,1)} all-to-all(bf16[32,40,128]{2,1,0:T(8,128)(2,1)} %bitcast.15), channel_id=1, replica_groups=mesh['y'=4,'zh'=2,'zl'=8,'x'=4,'core'=2] {'y','x','core'}, dimensions={0} | all-to-all | bytes 655360 | tf_op jit(solution)/shard_map/all_to_all | solution.py:336
  46.0 1.7 %sum_1.1 = bf16[16,24,128]{2,1,0:T(8,128)(2,1)} custom-call(bf16[32,40,128]{2,1,0:T(8,128)(2,1)} %all_to_all.15.in_ref), custom_call_target="tpu_custom_call" | custom-call | bytes 1048576 | tf_op jit(solution)/shard_map/sum_1/pallas_call | solution.py:360
  47.7 28.0 %all_to_all.16.in_ref = bf16[16,24,128]{2,1,0:T(8,128)(2,1)} all-to-all(bf16[16,24,128]{2,1,0:T(8,128)(2,1)} %sum_1.1), channel_id=1, replica_groups=mesh['y'=4,'zh'=2,'zl'=8,'x'=4,'core'=2] {'zh','zl'}, dimensions={0} | all-to-all | bytes 196608 | tf_op jit(solution)/shard_map/all_to_all | solution.py:336
  75.7 1.6 %sum_2.1 = f32[8,24,128]{2,1,0:T(8,128)} custom-call(bf16[16,24,128]{2,1,0:T(8,128)(2,1)} %all_to_all.16.in_ref), custom_call_target="tpu_custom_call" | custom-call | bytes 1048576 | tf_op jit(solution)/shard_map/sum_2/pallas_call | solution.py:362
  77.3 5.8 %all-to-all-start.2 = ((f32[8,24,128]{2,1,0:T(8,128)}), f32[8,24,128]{2,1,0:T(8,128)S(1)}, u32[]{:S(2)}, u32[]{:S(2)}) async-start(f32[8,24,128]{2,1,0:T(8,128)} %sum_2.1), calls=%async_computation.2 | async-start | bytes 196608 | tf_op jit(solution)/shard_map/all_to_all | solution.py:336
  83.1 2.6 %features_back.1 = bf16[4,256,128]{2,1,0:T(8,128)(2,1)} custom-call(bf16[6,256,128]{2,1,0:T(8,128)(2,1)} %get-tuple-element.14.grad_ref, bf16[3,3,128,128]{3,2,1,0:T(8,128)(2,1)} %conv_ref.3), custom_call_target="tpu_custom_call" | custom-call | flops 1073741824 | bytes 1048576 | tf_op jit(solution)/shard_map/features_back/pallas_call | solution.py:325
  85.6 2.4 %all-to-all-done.2.in_ref = f32[8,24,128]{2,1,0:T(8,128)S(1)} async-done(((f32[8,24,128]{2,1,0:T(8,128)}), f32[8,24,128]{2,1,0:T(8,128)S(1)}, u32[]{:S(2)}, u32[]{:S(2)}) %all-to-all-start.2) | async-done | bytes 98336 | tf_op jit(solution)/shard_map/all_to_all | solution.py:336
  88.1 0.0 copy-start
  88.1 0.6 copy-done
  88.7 1.5 %join.1 = (f32[144,128]{1,0:T(8,128)}, f32[3,16]{1,0:T(4,128)}) custom-call(f32[8,24,128]{2,1,0:T(8,128)} %copy-done), custom_call_target="tpu_custom_call" | custom-call | bytes 1048576 | tf_op jit(solution)/shard_map/join/pallas_call | solution.py:364
  (2 shorter events, 0.0 us)
Async XLA Ops:
  0.6 16.4 %copy-start.3 = (f32[64]{0:T(128)S(1)}, f32[64]{0:T(128)}, u32[]{:S(2)}) copy-start(f32[64]{0:T(128)} %param.17) | copy-start | bytes 772
  0.6 16.4 %copy-start.4 = (f32[64]{0:T(128)S(1)}, f32[64]{0:T(128)}, u32[]{:S(2)}) copy-start(f32[64]{0:T(128)} %param.15) | copy-start | bytes 772
  0.7 21.6 %collective-permute-start.3 = (f32[3,4,256]{2,1,0:T(4,128)}, f32[3,4,256]{2,1,0:T(4,128)S(1)}, u32[]{:S(2)}, u32[]{:S(2)}) collective-permute-start(f32[3,4,256]{2,1,0:T(4,128)} %bitcast.21), channel_id=1, source_target_pairs={{1,0},{2,1},{3,2},{4,3},{5,4},{6,5},{7,6},{8,7},{9,8},{10,9},{11,1... | collective-permute-start | bytes 36872 | tf_op jit(solution)/shard_map/ppermute | solution.py:350
  9.5 12.7 %collective-permute-start.2 = (f32[3,4,256]{2,1,0:T(4,128)}, f32[3,4,256]{2,1,0:T(4,128)S(1)}, u32[]{:S(2)}, u32[]{:S(2)}) collective-permute-start(f32[3,4,256]{2,1,0:T(4,128)} %bitcast.22), channel_id=1, source_target_pairs={{0,1},{1,2},{2,3},{3,4},{4,5},{5,6},{6,7},{7,8},{8,9},{9,10},{10,1... | collective-permute-start | bytes 36872 | tf_op jit(solution)/shard_map/ppermute | solution.py:350
  11.5 10.8 %collective-permute-start.1 = (bf16[4,256,128]{2,1,0:T(8,128)(2,1)}, bf16[4,256,128]{2,1,0:T(8,128)(2,1)S(1)}, u32[]{:S(2)}, u32[]{:S(2)}) collective-permute-start(bf16[4,256,128]{2,1,0:T(8,128)(2,1)} %bitcast.17), channel_id=1, source_target_pairs={{1,0},{2,1},{3,2},{4,3},{5,4},{6,5},{7,6},{8,7},{9,8},{10,9},{11,1... | collective-permute-start | bytes 786440 | tf_op jit(solution)/shard_map/ppermute | solution.py:349
  13.9 8.4 %collective-permute-start = (bf16[4,256,128]{2,1,0:T(8,128)(2,1)}, bf16[4,256,128]{2,1,0:T(8,128)(2,1)S(1)}, u32[]{:S(2)}, u32[]{:S(2)}) collective-permute-start(bf16[4,256,128]{2,1,0:T(8,128)(2,1)} %bitcast.18), channel_id=1, source_target_pairs={{0,1},{1,2},{2,3},{3,4},{4,5},{5,6},{6,7},{7,8},{8,9},{9,10},{10,1... | collective-permute-start | bytes 786440 | tf_op jit(solution)/shard_map/ppermute | solution.py:349
  17.1 0.8 copy-start.1
  17.9 0.7 copy-start.2
  22.3 0.8 copy-start.7
  22.3 0.8 copy-start.8
  22.3 0.8 copy-start.5
  22.3 0.8 copy-start.6
  77.3 10.8 %all-to-all-start.2 = ((f32[8,24,128]{2,1,0:T(8,128)}), f32[8,24,128]{2,1,0:T(8,128)S(1)}, u32[]{:S(2)}, u32[]{:S(2)}) async-start(f32[8,24,128]{2,1,0:T(8,128)} %sum_2.1), calls=%async_computation.2 | async-start | bytes 196608 | tf_op jit(solution)/shard_map/all_to_all | solution.py:336
  88.1 0.6 copy-start

commit v2 on v1

--- a/solution.py
+++ b/solution.py
@@ -16,6 +16,7 @@
 
 ROWS_LOC = 4
 COLS = 256
+TILE = ROWS_LOC * COLS
 CH = 128
 TILES = 64
 HEIGHT = ROWS_LOC * TILES
@@ -59,7 +60,28 @@
     return jnp.where(lane == COLS - 1, 0.0, pltpu.roll(x, COLS - 1, 1))
 
 
-def prep_kernel(w27_ref, ahead_ref, back_ref, band_ref, band_t_ref):
+def pack_kernel(own_ref, truth_ref, out_ref, sem):
+    copy = pltpu.make_async_copy(own_ref, out_ref.at[pl.ds(0, TILE)], sem)
+    copy.start()
+    rows = [
+        truth_ref[c, :, h * CH : (h + 1) * CH] for c in range(3) for h in range(COLS // CH)
+    ] + [jnp.zeros((8, CH), jnp.float32)]
+    exact = jnp.concatenate(rows, axis=0)
+    high = exact.astype(jnp.bfloat16)
+    out_ref[pl.ds(TILE, 32), :] = high
+    out_ref[pl.ds(TILE + 32, 32), :] = (exact - high.astype(jnp.float32)).astype(jnp.bfloat16)
+    copy.wait()
+
+
+def prep_kernel(
+    disc_ref, lpips_ref, head_ref, lin_ref, out_w_ref, ahead_ref, back_ref,
+    band_ref, band_t_ref, heads_ref, wide_ref, w27_ref,
+):
+    w27_ref[...] = jnp.zeros_like(w27_ref)
+    for a in range(3):
+        for b in range(3):
+            pair = jnp.concatenate([disc_ref[a, b], lpips_ref[a, b]], axis=1)
+            w27_ref[pl.ds((a * 3 + b) * 3, 3), :] = pair
     w27 = w27_ref[...].astype(jnp.bfloat16)
     size = 3 * N_GRAD * 8
     for r in range(N_LOSS):
@@ -67,10 +89,14 @@
         band_ref[r * CH : (r + 1) * CH, :] = band.astype(jnp.bfloat16)
         back = dot(back_ref[r * size : (r + 1) * size, :], w27, 1, 0)
         band_t_ref[:, r * CH : (r + 1) * CH] = back.astype(jnp.bfloat16)
+    line = jnp.concatenate([-ADV_SCALE * head_ref[...], 2.0 * lin_ref[...]], axis=1)
+    heads_ref[...] = jnp.broadcast_to(line, (CH, CH)).T
+    wide_ref[...] = jnp.zeros_like(wide_ref)
+    wide_ref[0:3, :] = out_w_ref[...].astype(jnp.float32)
 
 
 def main_kernel(
-    tile_ref, up_ref, own_ref, down_ref, t_up_ref, t_own_ref, t_down_ref, conv_ref, out_w_ref,
+    tile_ref, up_ref, own_ref, down_ref, conv_ref, out_w_ref,
     band_ref, band_t_ref, heads_ref,
     recon_ref, grad_pre_ref, piece_ref,
     y0, y1, y2, slope, hidden, truth, dall, packed,
@@ -83,7 +109,7 @@
         return jnp.where(inside, 1.0, 0.0).astype(f32)
 
     def feats(j):
-        return (up_ref, own_ref, down_ref)[j // ROWS_LOC][j % ROWS_LOC]
+        return (up_ref, own_ref, down_ref)[j // ROWS_LOC][pl.ds(j % ROWS_LOC * COLS, COLS), :]
 
     for buf in (y0, y2):
         for j in range(N_PRE + 1):
@@ -115,11 +141,16 @@
     image = jnp.concatenate(image, axis=0)
 
     truth[...] = jnp.zeros_like(truth)
+    targets = [
+        ref[pl.ds(TILE, 32), :].astype(f32) + ref[pl.ds(TILE + 32, 32), :].astype(f32)
+        for ref in (up_ref, own_ref, down_ref)
+    ]
     for j in range(N_PRE):
-        k = j + 1
-        src = (t_up_ref, t_own_ref, t_down_ref)[k // ROWS_LOC]
+        src, row = targets[(j + 1) // ROWS_LOC], (j + 1) % ROWS_LOC
         for c in range(3):
-            truth[j * 8 + c : j * 8 + c + 1, :] = src[c, k % ROWS_LOC : k % ROWS_LOC + 1, :]
+            for h in range(COLS // CH):
+                at = (c * 2 + h) * ROWS_LOC + row
+                truth[j * 8 + c : j * 8 + c + 1, h * CH : (h + 1) * CH] = src[at : at + 1]
     true_image = truth[...]
 
     def taps(x):
@@ -251,9 +282,10 @@
         out_ref[c : c + 1, :] = in_ref[c, 18:19, :16]
 
 
-def call(kernel, out_shape, scratch=(), smem=0, n_in=1, flops=0, name=None):
+def call(kernel, out_shape, scratch=(), smem=0, whole=0, n_in=1, flops=0, name=None, vmem=4):
     specs = [pl.BlockSpec(memory_space=pltpu.SMEM)] * smem
-    specs += [pl.BlockSpec(memory_space=VMEM)] * (n_in - smem)
+    specs += [pl.BlockSpec(memory_space=pl.ANY)] * whole
+    specs += [pl.BlockSpec(memory_space=VMEM)] * (n_in - smem - whole)
     many = isinstance(out_shape, tuple)
     return pl.pallas_call(
         kernel,
@@ -264,6 +296,7 @@
         else pl.BlockSpec(memory_space=VMEM),
         scratch_shapes=list(scratch),
         cost_estimate=pl.CostEstimate(flops=flops, bytes_accessed=1 << 20, transcendentals=0),
+        compiler_params=pltpu.CompilerParams(vmem_limit_bytes=vmem << 20),
         name=name,
     )
 
@@ -272,28 +305,39 @@
     return jax.ShapeDtypeStruct(dims, dtype)
 
 
+def pack(features, targets):
+    return call(
+        pack_kernel,
+        shape(TILE + 64, CH, dtype=jnp.bfloat16),
+        scratch=[pltpu.SemaphoreType.DMA],
+        n_in=2,
+        whole=1,
+        name="pack",
+    )(features.reshape(TILE, CH), targets)
+
+
 def prepare(disc_weight, disc_head, lpips_weight, lpips_lin, out_weight):
-    f32 = jnp.float32
+    bf16 = jnp.bfloat16
     ahead, back = band_selectors()
-    w27 = jnp.concatenate([disc_weight.reshape(27, 64), lpips_weight.reshape(27, 64)], axis=1)
-    w27 = jnp.pad(w27, ((0, 5), (0, 0)))
-    heads = jnp.concatenate([-ADV_SCALE * disc_head, 2.0 * lpips_lin])
-    heads = jnp.broadcast_to(heads[:, None], (128, 128))
-    out_w = jnp.pad(out_weight.astype(f32).T, ((0, 5), (0, 0)))
-    band, band_t = call(
+    return call(
         prep_kernel,
         (
-            shape(N_LOSS * CH, K_BAND, dtype=jnp.bfloat16),
-            shape(3 * N_GRAD * 8, N_LOSS * CH, dtype=jnp.bfloat16),
+            shape(N_LOSS * CH, K_BAND, dtype=bf16),
+            shape(3 * N_GRAD * 8, N_LOSS * CH, dtype=bf16),
+            shape(CH, CH),
+            shape(8, CH),
         ),
-        n_in=3,
+        scratch=[VMEM((32, CH), jnp.float32)],
+        n_in=7,
         flops=1 << 28,
         name="bands",
-    )(w27, jnp.asarray(ahead, jnp.bfloat16), jnp.asarray(back, jnp.bfloat16))
-    return band, band_t, heads, out_w
-
-
-def tile_step(tile, up, own, down, t_up, t_own, t_down, conv_weight, out_w, band, band_t, heads):
+    )(
+        disc_weight, lpips_weight, disc_head.reshape(1, -1), lpips_lin.reshape(1, -1),
+        out_weight.T, jnp.asarray(ahead, bf16), jnp.asarray(back, bf16),
+    )
+
+
+def tile_step(tile, up, own, down, conv_weight, band, band_t, heads, out_w):
     f32, bf16 = jnp.float32, jnp.bfloat16
     rows = N_PRE * PITCH + 8
     return call(
@@ -314,10 +358,11 @@
             VMEM((32 * 2 * BLOCK, CH), f32),
         ],
         smem=1,
-        n_in=12,
+        n_in=9,
         flops=1 << 31,
         name="tile",
-    )(tile, up, own, down, t_up, t_own, t_down, conv_weight, out_w, band, band_t, heads)
+        vmem=20,
+    )(tile, up, own, down, conv_weight, out_w, band, band_t, heads)
 
 
 def back_step(grad_pre, conv_weight):
@@ -329,6 +374,7 @@
         n_in=2,
         flops=1 << 30,
         name="features_back",
+        vmem=8,
     )(grad_pre, conv_weight)
 
 
@@ -342,19 +388,12 @@
 def body(
     features, conv_weight, out_weight, targets, disc_weight, disc_head, lpips_weight, lpips_lin
 ):
-    own = features[0]
-    t_own = jnp.transpose(targets[0], (2, 0, 1))
-    fall = [(i, i + 1) for i in range(TILES - 1)]
-    rise = [(i + 1, i) for i in range(TILES - 1)]
-    up, down = lax.ppermute(own, ROWS, fall), lax.ppermute(own, ROWS, rise)
-    t_up, t_down = lax.ppermute(t_own, ROWS, fall), lax.ppermute(t_own, ROWS, rise)
-    band, band_t, heads, out_w = prepare(
-        disc_weight, disc_head, lpips_weight, lpips_lin, out_weight
-    )
+    own = pack(features[0], jnp.transpose(targets[0], (2, 0, 1)))
+    up = lax.ppermute(own, ROWS, [(i, i + 1) for i in range(TILES - 1)])
+    down = lax.ppermute(own, ROWS, [(i + 1, i) for i in range(TILES - 1)])
+    tables = prepare(disc_weight, disc_head, lpips_weight, lpips_lin, out_weight)
     tile = lax.axis_index(ROWS).astype(jnp.int32).reshape(1)
-    recon, grad_pre, pieces = tile_step(
-        tile, up, own, down, t_up, t_own, t_down, conv_weight, out_w, band, band_t, heads
-    )
+    recon, grad_pre, pieces = tile_step(tile, up, own, down, conv_weight, *tables)
     grad_features = back_step(grad_pre, conv_weight)
     pieces = swap(pieces.reshape(32, 2 * BLOCK, CH), ("y", "x", "core"))
     pieces = call(first_sum_kernel, shape(16, PADDED, CH, dtype=jnp.bfloat16), name="sum_1")(pieces)

time: 90.9 us -> 75.8 us (0.83)
  Pallas kernels: 16.1 us -> 7.99 us
  starting transfers between devices: 22.2 us -> 16.6 us
  waiting for transfers between devices: 2.45 us -> 5.73 us
  blocking collectives: 44.5 us -> 42 us
  other arithmetic: 1.35 us -> 0 us
    ppermute x4 -> x2, starting transfers between devices: 16.4 us -> 10.8 us  [the longest x1 8.88 us: body(): down = lax.ppermute(own, ROWS, [(i + 1, i) for i in range(TILES - 1)])]
    all_to_all x2, blocking collectives: 44.5 us -> 42 us  [swap(): return lax.all_to_all(array, axes, split_axis=0, concat_axis=0, tiled=True)]
    ppermute x4 -> x2, waiting for transfers between devices: 0.01 us -> 2.21 us  [the longest x1 2.21 us: body(): up = lax.ppermute(own, ROWS, [(i, i + 1) for i in range(TILES - 1)])]
    pallas_call x1, Pallas kernels: 6.43 us -> 4.57 us  [tile_step(): call(main_kernel, (shape(3, ROWS_LOC, COLS), shape(N_GRAD, COLS, CH, dtyp...]
    pallas_call x1 -> x2, Pallas kernels: 2.37 us -> 0.57 us  [the longest x1 0.54 us: prepare(): call(prep_kernel, (shape(N_LOSS * CH, K_BAND, dtype=bf16), shape(3 * N_GR...]
    pallas_call x1, Pallas kernels: 1.67 us -> 0.06 us  [body(): call(first_sum_kernel, shape(16, PADDED, CH, dtype=jnp.bfloat16), name='s...]
    pallas_call x1, Pallas kernels: 2.56 us -> 1.48 us  [back_step(): call(back_kernel, shape(ROWS_LOC, COLS, CH, dtype=jnp.bfloat16), scratch=...]
    all_to_all x1, waiting for transfers between devices: 2.44 us -> 3.52 us  [swap(): return lax.all_to_all(array, axes, split_axis=0, concat_axis=0, tiled=True)]
  transfers between devices with their start and end apart: 5 -> 3, of which waited for: 1 -> 2; matrix products, arithmetic and copies ran while one was open for 2% -> 0% of each run, Pallas kernels for 5% -> 3%
where the time goes in v2:
time: 75.8 us; the launch traced here: 75.4 us
  blocking collectives  42 us (55%)
  starting transfers between devices  16.6 us (22%)
  Pallas kernels  7.99 us (11%)
  waiting for transfers between devices  5.73 us (8%)
  local copies, waits for them, and re-layouts  2.3 us (3%)
  between operations  0.76 us (1%)
    all_to_all x2, blocking collectives, swap(): return lax.all_to_all(array, axes, split_axis=0, concat_axis=0, tiled=True)  42 us
    ppermute x1, starting transfers between devices, body(): down = lax.ppermute(own, ROWS, [(i + 1, i) for i in range(TILES - 1)])  8.88 us
    all_to_all x1, starting transfers between devices, swap(): return lax.all_to_all(array, axes, split_axis=0, concat_axis=0, tiled=True)  5.79 us
    pallas_call x1, Pallas kernels, tile_step(): call(main_kernel, (shape(3, ROWS_LOC, COLS), shape(N_GRAD, COLS, CH, dtyp...  4.57 us
    all_to_all x1, waiting for transfers between devices, swap(): return lax.all_to_all(array, axes, split_axis=0, concat_axis=0, tiled=True)  3.52 us
    unnamed x20, local copies, waits for them, and re-layouts  2.3 us
    ppermute x1, waiting for transfers between devices, body(): up = lax.ppermute(own, ROWS, [(i, i + 1) for i in range(TILES - 1)])  2.21 us
    ppermute x1, starting transfers between devices, body(): up = lax.ppermute(own, ROWS, [(i, i + 1) for i in range(TILES - 1)])  1.92 us
  transfers between devices with their start and end apart: 3, of which 2 were waited for; matrix products, arithmetic and copies ran while one was open for 0% of the time, Pallas kernels for 3%

profile of v2, /device:TPU:1, one launch (start us, length us, event | category | flops | bytes accessed | tf_op | source)
XLA Modules:
  0.0 75.4 jit_solution(2345350956822468313)
XLA Ops:
  0.6 0.0 copy-start
  0.6 0.9 %copy-done = bf16[1,4,256,128]{3,2,1,0:T(8,128)(2,1)S(1)} copy-done((bf16[1,4,256,128]{3,2,1,0:T(8,128)(2,1)S(1)}, bf16[1,4,256,128]{3,2,1,0:T(8,128)(2,1)}, u32[]{:S(2)}) %copy-start) | copy-done | bytes 262168
  1.6 0.0 copy-start.1
  1.6 0.7 copy-done.1
  2.3 0.0 copy-start.4
  2.3 0.0 copy-start.8
  2.3 0.0 copy-start.9
  2.3 0.0 copy-start.3
  2.4 8.9 %collective-permute-start.1 = (bf16[1088,128]{1,0:T(8,128)(2,1)S(1)}, bf16[1088,128]{1,0:T(8,128)(2,1)S(1)}, u32[]{:S(2)}, u32[]{:S(2)}) collective-permute-start(bf16[1088,128]{1,0:T(8,128)(2,1)S(1)} %pack.1.own_ref), channel_id=1, source_target_pairs={{1,0},{2,1},{3,2},{4,3},{5,4},{6,5},{7,6},{8,7},{9,8},{10,9},{11,1... | collective-permute-start | bytes 835592 | tf_op jit(solution)/shard_map/ppermute | solution.py:393
  11.2 1.9 %collective-permute-start = (bf16[1088,128]{1,0:T(8,128)(2,1)S(1)}, bf16[1088,128]{1,0:T(8,128)(2,1)S(1)}, u32[]{:S(2)}, u32[]{:S(2)}) collective-permute-start(bf16[1088,128]{1,0:T(8,128)(2,1)S(1)} %pack.1.own_ref), channel_id=1, source_target_pairs={{0,1},{1,2},{2,3},{3,4},{4,5},{5,6},{6,7},{7,8},{8,9},{9,10},{10,1... | collective-permute-start | bytes 835592 | tf_op jit(solution)/shard_map/ppermute | solution.py:392
  13.2 0.0 copy-start.7
  13.2 0.0 copy-start.5
  13.2 0.0 copy-start.6
  13.2 0.0 copy-done.4
  13.2 0.0 copy-done.8
  13.2 0.0 copy-done.9
  13.2 0.0 copy-done.3
  13.2 0.6 copy-done.7
  13.8 0.0 copy-done.5
  13.9 0.0 copy-done.6
  13.9 0.0 copy-start.2
  13.9 0.5 bands.1
  14.4 0.0 collective-permute-done.1.down_ref
  14.4 2.2 %collective-permute-done.up_ref = bf16[1088,128]{1,0:T(8,128)(2,1)S(1)} collective-permute-done((bf16[1088,128]{1,0:T(8,128)(2,1)S(1)}, bf16[1088,128]{1,0:T(8,128)(2,1)S(1)}, u32[]{:S(2)}, u32[]{:S(2)}) %collective-permute-start) | collective-permute-done | bytes 278560 | tf_op jit(solution)/shard_map/ppermute | solution.py:392
  16.6 0.0 copy-done.2
  16.6 4.6 %tile.1 = (f32[3,4,256]{2,1,0:T(4,128)}, bf16[6,256,128]{2,1,0:T(8,128)(2,1)S(1)}, bf16[1280,128]{1,0:T(8,128)(2,1)S(1)}) custom-call(s32[1]{0:T(128)} %bitcast.tile_ref, bf16[1088,128]{1,0:T(8,128)(2,1)S(1)} %collective-permute-done.up_ref, bf16[1088,128]{1,0:T(8,128)(2,1)S(1)} %pack.1.own_ref, bf16[1088,128]{1,0:T(8,128)(2,1)S(1)} %collective-permute-done.1.down_ref, ...), custom_call_target="tpu_custom_call" | custom-call | flops 2147483648 | bytes 1048576 | tf_op jit(solution)/shard_map/tile/pallas_call | solution.py:343
  21.2 14.1 %all_to_all.15.in_ref = bf16[32,40,128]{2,1,0:T(8,128)(2,1)S(1)} all-to-all(bf16[32,40,128]{2,1,0:T(8,128)(2,1)S(1)} %bitcast.17), channel_id=1, replica_groups=mesh['y'=4,'zh'=2,'zl'=8,'x'=4,'core'=2] {'y','x','core'}, dimensions={0} | all-to-all | bytes 655360 | tf_op jit(solution)/shard_map/all_to_all | solution.py:382
  35.3 0.1 sum_1.1
  35.3 27.9 %all_to_all.16.in_ref = bf16[16,24,128]{2,1,0:T(8,128)(2,1)S(1)} all-to-all(bf16[16,24,128]{2,1,0:T(8,128)(2,1)S(1)} %sum_1.1), channel_id=1, replica_groups=mesh['y'=4,'zh'=2,'zl'=8,'x'=4,'core'=2] {'zh','zl'}, dimensions={0} | all-to-all | bytes 196608 | tf_op jit(solution)/shard_map/all_to_all | solution.py:382
  63.3 0.7 sum_2.1
  63.9 5.8 %all-to-all-start.2 = ((f32[8,24,128]{2,1,0:T(8,128)}), f32[8,24,128]{2,1,0:T(8,128)S(1)}, u32[]{:S(2)}, u32[]{:S(2)}) async-start(f32[8,24,128]{2,1,0:T(8,128)} %sum_2.1), calls=%async_computation.2 | async-start | bytes 196608 | tf_op jit(solution)/shard_map/all_to_all | solution.py:382
  69.7 1.5 %features_back.1 = bf16[4,256,128]{2,1,0:T(8,128)(2,1)} custom-call(bf16[6,256,128]{2,1,0:T(8,128)(2,1)S(1)} %get-tuple-element.18.grad_ref, bf16[3,3,128,128]{3,2,1,0:T(8,128)(2,1)S(1)} %copy-done.2), custom_call_target="tpu_custom_call" | custom-call | flops 1073741824 | bytes 1048576 | tf_op jit(solution)/shard_map/features_back/pallas_call | solution.py:370
  71.2 3.5 %all-to-all-done.2.in_ref = f32[8,24,128]{2,1,0:T(8,128)S(1)} async-done(((f32[8,24,128]{2,1,0:T(8,128)}), f32[8,24,128]{2,1,0:T(8,128)S(1)}, u32[]{:S(2)}, u32[]{:S(2)}) %all-to-all-start.2) | async-done | bytes 98336 | tf_op jit(solution)/shard_map/all_to_all | solution.py:382
  74.7 0.6 join.1
  (1 shorter events, 0.0 us)
Async XLA Ops:
  0.6 1.0 %copy-start = (bf16[1,4,256,128]{3,2,1,0:T(8,128)(2,1)S(1)}, bf16[1,4,256,128]{3,2,1,0:T(8,128)(2,1)}, u32[]{:S(2)}) copy-start(bf16[1,4,256,128]{3,2,1,0:T(8,128)(2,1)} %param.10) | copy-start | bytes 786436
  1.6 0.7 copy-start.1
  2.3 10.9 %copy-start.4 = (f32[3,3,3,64]{3,2,1,0:T(4,128)S(1)}, f32[3,3,3,64]{3,2,1,0:T(4,128)}, u32[]{:S(2)}) copy-start(f32[3,3,3,64]{3,2,1,0:T(4,128)} %lpips_ref.1) | copy-start | bytes 20740
  2.3 10.9 %copy-start.8 = (bf16[1152,32]{1,0:T(8,128)(2,1)S(1)}, bf16[1152,32]{1,0:T(8,128)(2,1)}, u32[]{:S(2)}) copy-start(bf16[1152,32]{1,0:T(8,128)(2,1)} %constant.21.clone.back_ref) | copy-start | bytes 221188
  2.3 10.9 %copy-start.9 = (bf16[32,2048]{1,0:T(8,128)(2,1)S(1)}, bf16[32,2048]{1,0:T(8,128)(2,1)}, u32[]{:S(2)}) copy-start(bf16[32,2048]{1,0:T(8,128)(2,1)} %constant.20.clone.ahead_ref) | copy-start | bytes 393220
  2.3 10.9 %copy-start.3 = (f32[3,3,3,64]{3,2,1,0:T(4,128)S(1)}, f32[3,3,3,64]{3,2,1,0:T(4,128)}, u32[]{:S(2)}) copy-start(f32[3,3,3,64]{3,2,1,0:T(4,128)} %disc_ref.1) | copy-start | bytes 20740
  2.4 12.1 %collective-permute-start.1 = (bf16[1088,128]{1,0:T(8,128)(2,1)S(1)}, bf16[1088,128]{1,0:T(8,128)(2,1)S(1)}, u32[]{:S(2)}, u32[]{:S(2)}) collective-permute-start(bf16[1088,128]{1,0:T(8,128)(2,1)S(1)} %pack.1.own_ref), channel_id=1, source_target_pairs={{1,0},{2,1},{3,2},{4,3},{5,4},{6,5},{7,6},{8,7},{9,8},{10,9},{11,1... | collective-permute-start | bytes 835592 | tf_op jit(solution)/shard_map/ppermute | solution.py:393
  11.2 5.4 %collective-permute-start = (bf16[1088,128]{1,0:T(8,128)(2,1)S(1)}, bf16[1088,128]{1,0:T(8,128)(2,1)S(1)}, u32[]{:S(2)}, u32[]{:S(2)}) collective-permute-start(bf16[1088,128]{1,0:T(8,128)(2,1)S(1)} %pack.1.own_ref), channel_id=1, source_target_pairs={{0,1},{1,2},{2,3},{3,4},{4,5},{5,6},{6,7},{7,8},{8,9},{9,10},{10,1... | collective-permute-start | bytes 835592 | tf_op jit(solution)/shard_map/ppermute | solution.py:392
  13.2 0.7 copy-start.7
  13.2 0.7 copy-start.5
  13.2 0.7 copy-start.6
  13.9 2.8 %copy-start.2 = (bf16[3,3,128,128]{3,2,1,0:T(8,128)(2,1)S(1)}, bf16[3,3,128,128]{3,2,1,0:T(8,128)(2,1)}, u32[]{:S(2)}) copy-start(bf16[3,3,128,128]{3,2,1,0:T(8,128)(2,1)} %conv_ref.3) | copy-start | bytes 884740
  63.9 10.8 %all-to-all-start.2 = ((f32[8,24,128]{2,1,0:T(8,128)}), f32[8,24,128]{2,1,0:T(8,128)S(1)}, u32[]{:S(2)}, u32[]{:S(2)}) async-start(f32[8,24,128]{2,1,0:T(8,128)} %sum_2.1), calls=%async_computation.2 | async-start | bytes 196608 | tf_op jit(solution)/shard_map/all_to_all | solution.py:382

commit v3 on v2

--- a/solution.py
+++ b/solution.py
@@ -60,11 +60,14 @@
     return jnp.where(lane == COLS - 1, 0.0, pltpu.roll(x, COLS - 1, 1))
 
 
-def pack_kernel(own_ref, truth_ref, out_ref, sem):
-    copy = pltpu.make_async_copy(own_ref, out_ref.at[pl.ds(0, TILE)], sem)
+def pack_kernel(own_ref, truth_ref, out_ref, truth_vmem, sems):
+    copy = pltpu.make_async_copy(own_ref, out_ref.at[pl.ds(0, TILE)], sems.at[0])
     copy.start()
+    fetch = pltpu.make_async_copy(truth_ref, truth_vmem, sems.at[1])
+    fetch.start()
+    fetch.wait()
     rows = [
-        truth_ref[c, :, h * CH : (h + 1) * CH] for c in range(3) for h in range(COLS // CH)
+        truth_vmem[c, :, h * CH : (h + 1) * CH] for c in range(3) for h in range(COLS // CH)
     ] + [jnp.zeros((8, CH), jnp.float32)]
     exact = jnp.concatenate(rows, axis=0)
     high = exact.astype(jnp.bfloat16)
@@ -96,12 +99,23 @@
 
 
 def main_kernel(
-    tile_ref, up_ref, own_ref, down_ref, conv_ref, out_w_ref,
+    tile_ref, near_ref, own_ref, far_ref, conv_ref, out_w_ref,
     band_ref, band_t_ref, heads_ref,
     recon_ref, grad_pre_ref, piece_ref,
-    y0, y1, y2, slope, hidden, truth, dall, packed,
+    y0, y1, y2, slope, hidden, truth, dall, packed, up_ref, down_ref,
 ):
     bf16, f32 = jnp.bfloat16, jnp.float32
+
+    @pl.when(lax.rem(tile_ref[0], 2) == 0)
+    def _():
+        up_ref[...] = far_ref[...]
+        down_ref[...] = near_ref[...]
+
+    @pl.when(lax.rem(tile_ref[0], 2) == 1)
+    def _():
+        up_ref[...] = near_ref[...]
+        down_ref[...] = far_ref[...]
+
     first_row = tile_ref[0] * ROWS_LOC
 
     def valid(row):
@@ -284,7 +298,7 @@
 
 def call(kernel, out_shape, scratch=(), smem=0, whole=0, n_in=1, flops=0, name=None, vmem=4):
     specs = [pl.BlockSpec(memory_space=pltpu.SMEM)] * smem
-    specs += [pl.BlockSpec(memory_space=pl.ANY)] * whole
+    specs += [pl.BlockSpec(memory_space=pltpu.HBM)] * whole
     specs += [pl.BlockSpec(memory_space=VMEM)] * (n_in - smem - whole)
     many = isinstance(out_shape, tuple)
     return pl.pallas_call(
@@ -309,11 +323,14 @@
     return call(
         pack_kernel,
         shape(TILE + 64, CH, dtype=jnp.bfloat16),
-        scratch=[pltpu.SemaphoreType.DMA],
+        scratch=[VMEM((3, ROWS_LOC, COLS), jnp.float32), pltpu.SemaphoreType.DMA((2,))],
         n_in=2,
-        whole=1,
+        whole=2,
         name="pack",
-    )(features.reshape(TILE, CH), targets)
+    )(
+        pltpu.with_memory_space_constraint(features.reshape(TILE, CH), pltpu.HBM),
+        pltpu.with_memory_space_constraint(targets, pltpu.HBM),
+    )
 
 
 def prepare(disc_weight, disc_head, lpips_weight, lpips_lin, out_weight):
@@ -337,7 +354,7 @@
     )
 
 
-def tile_step(tile, up, own, down, conv_weight, band, band_t, heads, out_w):
+def tile_step(tile, near, own, far, conv_weight, band, band_t, heads, out_w):
     f32, bf16 = jnp.float32, jnp.bfloat16
     rows = N_PRE * PITCH + 8
     return call(
@@ -356,13 +373,15 @@
             VMEM((N_PRE * 8, COLS), f32),
             VMEM((N_LOSS * CH, COLS), bf16),
             VMEM((32 * 2 * BLOCK, CH), f32),
+            VMEM((TILE + 64, CH), bf16),
+            VMEM((TILE + 64, CH), bf16),
         ],
         smem=1,
         n_in=9,
         flops=1 << 31,
         name="tile",
         vmem=20,
-    )(tile, up, own, down, conv_weight, out_w, band, band_t, heads)
+    )(tile, near, own, far, conv_weight, out_w, band, band_t, heads)
 
 
 def back_step(grad_pre, conv_weight):
@@ -382,6 +401,10 @@
     return lax.all_to_all(array, axes, split_axis=0, concat_axis=0, tiled=True)
 
 
+def swaps(firsts):
+    return [pair for i in firsts for pair in ((i, i + 1), (i + 1, i))]
+
+
 ROWS = ("zl", "x", "core")
 
 
@@ -389,11 +412,11 @@
     features, conv_weight, out_weight, targets, disc_weight, disc_head, lpips_weight, lpips_lin
 ):
     own = pack(features[0], jnp.transpose(targets[0], (2, 0, 1)))
-    up = lax.ppermute(own, ROWS, [(i, i + 1) for i in range(TILES - 1)])
-    down = lax.ppermute(own, ROWS, [(i + 1, i) for i in range(TILES - 1)])
+    near = lax.ppermute(own, ROWS, swaps(range(0, TILES, 2)))
+    far = lax.ppermute(own, ROWS, swaps(range(1, TILES - 1, 2)))
     tables = prepare(disc_weight, disc_head, lpips_weight, lpips_lin, out_weight)
     tile = lax.axis_index(ROWS).astype(jnp.int32).reshape(1)
-    recon, grad_pre, pieces = tile_step(tile, up, own, down, conv_weight, *tables)
+    recon, grad_pre, pieces = tile_step(tile, near, own, far, conv_weight, *tables)
     grad_features = back_step(grad_pre, conv_weight)
     pieces = swap(pieces.reshape(32, 2 * BLOCK, CH), ("y", "x", "core"))
     pieces = call(first_sum_kernel, shape(16, PADDED, CH, dtype=jnp.bfloat16), name="sum_1")(pieces)

time: 75.8 us -> 72.4 us (0.955)
  waiting for transfers between devices: 5.73 us -> 3.52 us
  starting transfers between devices: 16.6 us -> 15.2 us
  local copies, waits for them, and re-layouts: 2.3 us -> 1.05 us
  Pallas kernels: 7.99 us -> 8.82 us
    ppermute x2, waiting for transfers between devices: 2.21 us -> 0.01 us  [the longest x1 0.01 us: body(): far = lax.ppermute(own, ROWS, swaps(range(1, TILES - 1, 2)))]
    ppermute x2, starting transfers between devices: 10.8 us -> 9.43 us  [the longest x1 4.93 us: body(): near = lax.ppermute(own, ROWS, swaps(range(0, TILES, 2)))]
    unnamed x20 -> x16, local copies, waits for them, and re-layouts: 2.3 us -> 1.05 us
    pallas_call x1, Pallas kernels: 0.03 us -> 1.02 us  [pack(): call(pack_kernel, shape(TILE + 64, CH, dtype=jnp.bfloat16), scratch=[VMEM...]
  transfers between devices with their start and end apart: 3 -> 3, of which waited for: 2 -> 1; matrix products, arithmetic and copies ran while one was open for 0% -> 0% of each run, Pallas kernels for 3% -> 3%
where the time goes in v3:
time: 72.4 us; the launch traced here: 71.9 us
  blocking collectives  42.6 us (59%)
  starting transfers between devices  15.2 us (21%)
  Pallas kernels  8.82 us (12%)
  waiting for transfers between devices  3.52 us (5%)
  local copies, waits for them, and re-layouts  1.05 us (1%)
  between operations  0.78 us (1%)
    all_to_all x2, blocking collectives, swap(): return lax.all_to_all(array, axes, split_axis=0, concat_axis=0, tiled=True)  42.6 us
    all_to_all x1, starting transfers between devices, swap(): return lax.all_to_all(array, axes, split_axis=0, concat_axis=0, tiled=True)  5.79 us
    ppermute x1, starting transfers between devices, body(): near = lax.ppermute(own, ROWS, swaps(range(0, TILES, 2)))  4.93 us
    ppermute x1, starting transfers between devices, body(): far = lax.ppermute(own, ROWS, swaps(range(1, TILES - 1, 2)))  4.5 us
    pallas_call x1, Pallas kernels, tile_step(): call(main_kernel, (shape(3, ROWS_LOC, COLS), shape(N_GRAD, COLS, CH, dtyp...  4.42 us
    all_to_all x1, waiting for transfers between devices, swap(): return lax.all_to_all(array, axes, split_axis=0, concat_axis=0, tiled=True)  3.52 us
    pallas_call x1, Pallas kernels, back_step(): call(back_kernel, shape(ROWS_LOC, COLS, CH, dtype=jnp.bfloat16), scratch=...  1.49 us
  transfers between devices with their start and end apart: 3, of which 1 were waited for; matrix products, arithmetic and copies ran while one was open for 0% of the time, Pallas kernels for 3%

profile of v3, /device:TPU:1, one launch (start us, length us, event | category | flops | bytes accessed | tf_op | source)
XLA Modules:
  0.0 71.9 jit_solution(9594388831108779454)
XLA Ops:
  0.6 0.0 copy-start.6
  0.6 0.0 copy-start.2
  0.7 0.0 copy-start.7
  0.7 1.0 %pack.1.own_ref = bf16[1088,128]{1,0:T(8,128)(2,1)S(1)} custom-call(bf16[1024,128]{1,0:T(8,128)(2,1)} %bitcast.21, f32[3,4,256]{2,1,0:T(4,128)} %bitcast.22), custom_call_target="tpu_custom_call" | custom-call | bytes 1048576 | tf_op jit(solution)/shard_map/pack/pallas_call | solution.py:323
  1.7 0.0 copy-start.1
  1.7 4.5 %collective-permute-start.1 = (bf16[1088,128]{1,0:T(8,128)(2,1)S(1)}, bf16[1088,128]{1,0:T(8,128)(2,1)S(1)}, u32[]{:S(2)}, u32[]{:S(2)}) collective-permute-start(bf16[1088,128]{1,0:T(8,128)(2,1)S(1)} %pack.1.own_ref), channel_id=1, source_target_pairs={{1,2},{2,1},{3,4},{4,3},{5,6},{6,5},{7,8},{8,7},{9,10},{10,9},{11,... | collective-permute-start | bytes 835592 | tf_op jit(solution)/shard_map/ppermute | solution.py:416
  6.2 4.9 %collective-permute-start = (bf16[1088,128]{1,0:T(8,128)(2,1)S(1)}, bf16[1088,128]{1,0:T(8,128)(2,1)S(1)}, u32[]{:S(2)}, u32[]{:S(2)}) collective-permute-start(bf16[1088,128]{1,0:T(8,128)(2,1)S(1)} %pack.1.own_ref), channel_id=1, source_target_pairs={{0,1},{1,0},{2,3},{3,2},{4,5},{5,4},{6,7},{7,6},{8,9},{9,8},{10,11... | collective-permute-start | bytes 835592 | tf_op jit(solution)/shard_map/ppermute | solution.py:415
  11.1 0.0 copy-start.5
  11.2 0.0 copy-start.3
  11.2 0.0 copy-start.4
  11.2 0.0 copy-done.6
  11.2 0.0 copy-done.2
  11.2 0.0 copy-done.7
  11.2 0.0 copy-done.1
  11.2 0.6 copy-done.5
  11.8 0.0 copy-done.3
  11.8 0.0 copy-done.4
  11.8 0.0 copy-start
  11.9 0.5 bands.1
  12.4 0.0 collective-permute-done.1.far_ref
  12.4 0.0 collective-permute-done.near_ref
  12.4 0.4 copy-done
  12.8 4.4 %tile.1 = (f32[3,4,256]{2,1,0:T(4,128)}, bf16[6,256,128]{2,1,0:T(8,128)(2,1)S(1)}, bf16[1280,128]{1,0:T(8,128)(2,1)S(1)}) custom-call(s32[1]{0:T(128)} %bitcast.tile_ref, bf16[1088,128]{1,0:T(8,128)(2,1)S(1)} %collective-permute-done.near_ref, bf16[1088,128]{1,0:T(8,128)(2,1)S(1)} %pack.1.own_ref, bf16[1088,128]{1,0:T(8,128)(2,1)S(1)} %collective-permute-done.1.far_ref, ...), custom_call_target="tpu_custom_call" | custom-call | flops 2147483648 | bytes 1048576 | tf_op jit(solution)/shard_map/tile/pallas_call | solution.py:360
  17.2 15.9 %all_to_all.15.in_ref = bf16[32,40,128]{2,1,0:T(8,128)(2,1)S(1)} all-to-all(bf16[32,40,128]{2,1,0:T(8,128)(2,1)S(1)} %bitcast.17), channel_id=1, replica_groups=mesh['y'=4,'zh'=2,'zl'=8,'x'=4,'core'=2] {'y','x','core'}, dimensions={0} | all-to-all | bytes 655360 | tf_op jit(solution)/shard_map/all_to_all | solution.py:401
  33.2 0.1 sum_1.1
  33.2 26.6 %all_to_all.16.in_ref = bf16[16,24,128]{2,1,0:T(8,128)(2,1)S(1)} all-to-all(bf16[16,24,128]{2,1,0:T(8,128)(2,1)S(1)} %sum_1.1), channel_id=1, replica_groups=mesh['y'=4,'zh'=2,'zl'=8,'x'=4,'core'=2] {'zh','zl'}, dimensions={0} | all-to-all | bytes 196608 | tf_op jit(solution)/shard_map/all_to_all | solution.py:401
  59.9 0.7 sum_2.1
  60.5 5.8 %all-to-all-start.2 = ((f32[8,24,128]{2,1,0:T(8,128)}), f32[8,24,128]{2,1,0:T(8,128)S(1)}, u32[]{:S(2)}, u32[]{:S(2)}) async-start(f32[8,24,128]{2,1,0:T(8,128)} %sum_2.1), calls=%async_computation.2 | async-start | bytes 196608 | tf_op jit(solution)/shard_map/all_to_all | solution.py:401
  66.3 1.5 %features_back.1 = bf16[4,256,128]{2,1,0:T(8,128)(2,1)} custom-call(bf16[6,256,128]{2,1,0:T(8,128)(2,1)S(1)} %get-tuple-element.18.grad_ref, bf16[3,3,128,128]{3,2,1,0:T(8,128)(2,1)S(1)} %copy-done), custom_call_target="tpu_custom_call" | custom-call | flops 1073741824 | bytes 1048576 | tf_op jit(solution)/shard_map/features_back/pallas_call | solution.py:389
  67.8 3.5 %all-to-all-done.2.in_ref = f32[8,24,128]{2,1,0:T(8,128)S(1)} async-done(((f32[8,24,128]{2,1,0:T(8,128)}), f32[8,24,128]{2,1,0:T(8,128)S(1)}, u32[]{:S(2)}, u32[]{:S(2)}) %all-to-all-start.2) | async-done | bytes 98336 | tf_op jit(solution)/shard_map/all_to_all | solution.py:401
  71.3 0.6 join.1
Async XLA Ops:
  0.6 10.6 %copy-start.6 = (bf16[1152,32]{1,0:T(8,128)(2,1)S(1)}, bf16[1152,32]{1,0:T(8,128)(2,1)}, u32[]{:S(2)}) copy-start(bf16[1152,32]{1,0:T(8,128)(2,1)} %constant.21.clone.back_ref) | copy-start | bytes 221188
  0.6 10.6 %copy-start.2 = (f32[3,3,3,64]{3,2,1,0:T(4,128)S(1)}, f32[3,3,3,64]{3,2,1,0:T(4,128)}, u32[]{:S(2)}) copy-start(f32[3,3,3,64]{3,2,1,0:T(4,128)} %lpips_ref.1) | copy-start | bytes 20740
  0.7 10.6 %copy-start.7 = (bf16[32,2048]{1,0:T(8,128)(2,1)S(1)}, bf16[32,2048]{1,0:T(8,128)(2,1)}, u32[]{:S(2)}) copy-start(bf16[32,2048]{1,0:T(8,128)(2,1)} %constant.20.clone.ahead_ref) | copy-start | bytes 393220
  1.7 9.5 %copy-start.1 = (f32[3,3,3,64]{3,2,1,0:T(4,128)S(1)}, f32[3,3,3,64]{3,2,1,0:T(4,128)}, u32[]{:S(2)}) copy-start(f32[3,3,3,64]{3,2,1,0:T(4,128)} %disc_ref.1) | copy-start | bytes 20740
  1.7 10.7 %collective-permute-start.1 = (bf16[1088,128]{1,0:T(8,128)(2,1)S(1)}, bf16[1088,128]{1,0:T(8,128)(2,1)S(1)}, u32[]{:S(2)}, u32[]{:S(2)}) collective-permute-start(bf16[1088,128]{1,0:T(8,128)(2,1)S(1)} %pack.1.own_ref), channel_id=1, source_target_pairs={{1,2},{2,1},{3,4},{4,3},{5,6},{6,5},{7,8},{8,7},{9,10},{10,9},{11,... | collective-permute-start | bytes 835592 | tf_op jit(solution)/shard_map/ppermute | solution.py:416
  6.2 6.2 %collective-permute-start = (bf16[1088,128]{1,0:T(8,128)(2,1)S(1)}, bf16[1088,128]{1,0:T(8,128)(2,1)S(1)}, u32[]{:S(2)}, u32[]{:S(2)}) collective-permute-start(bf16[1088,128]{1,0:T(8,128)(2,1)S(1)} %pack.1.own_ref), channel_id=1, source_target_pairs={{0,1},{1,0},{2,3},{3,2},{4,5},{5,4},{6,7},{7,6},{8,9},{9,8},{10,11... | collective-permute-start | bytes 835592 | tf_op jit(solution)/shard_map/ppermute | solution.py:415
  11.1 0.7 copy-start.5
  11.2 0.7 copy-start.3
  11.2 0.7 copy-start.4
  11.8 1.0 %copy-start = (bf16[3,3,128,128]{3,2,1,0:T(8,128)(2,1)S(1)}, bf16[3,3,128,128]{3,2,1,0:T(8,128)(2,1)}, u32[]{:S(2)}) copy-start(bf16[3,3,128,128]{3,2,1,0:T(8,128)(2,1)} %conv_ref.3) | copy-start | bytes 884740
  60.5 10.8 %all-to-all-start.2 = ((f32[8,24,128]{2,1,0:T(8,128)}), f32[8,24,128]{2,1,0:T(8,128)S(1)}, u32[]{:S(2)}, u32[]{:S(2)}) async-start(f32[8,24,128]{2,1,0:T(8,128)} %sum_2.1), calls=%async_computation.2 | async-start | bytes 196608 | tf_op jit(solution)/shard_map/all_to_all | solution.py:401

commit v4 on v3

--- a/solution.py
+++ b/solution.py
@@ -251,20 +251,20 @@
     piece_ref[...] = packed[...].astype(bf16)
 
 
-def back_kernel(grad_ref, conv_ref, out_ref, z0, z1, z2):
+def back_kernel(start, grad_ref, conv_ref, out_ref, z0, z1, z2):
     bf16, f32 = jnp.bfloat16, jnp.float32
     for buf in (z0, z2):
-        for y in range(ROWS_LOC + 1):
+        for y in range(out_ref.shape[0] + 1):
             buf[pl.ds(y * PITCH, 8), :] = jnp.zeros((8, CH), f32)
     weights = jnp.concatenate(
         [jnp.concatenate([conv_ref[a, b] for a in range(3)], axis=1) for b in range(3)], axis=0
     )
-    for y in range(ROWS_LOC):
-        lhs = jnp.concatenate([grad_ref[y + 2 - a] for a in range(3)], axis=1)
+    for y in range(out_ref.shape[0]):
+        lhs = jnp.concatenate([grad_ref[start + y + 2 - a] for a in range(3)], axis=1)
         prod = dot(lhs, weights, 1, 1)
         for b, buf in enumerate((z0, z1, z2)):
             buf[pl.ds(y * PITCH + 8, COLS), :] = prod[:, b * CH : (b + 1) * CH]
-    for y in range(ROWS_LOC):
+    for y in range(out_ref.shape[0]):
         at = y * PITCH + 8
         total = z0[pl.ds(at + 1, COLS), :] + z1[pl.ds(at, COLS), :] + z2[pl.ds(at - 1, COLS), :]
         out_ref[y] = total.astype(bf16)
@@ -384,11 +384,11 @@
     )(tile, near, own, far, conv_weight, out_w, band, band_t, heads)
 
 
-def back_step(grad_pre, conv_weight):
-    rows = ROWS_LOC * PITCH + 8
+def back_step(start, count, grad_pre, conv_weight):
+    rows = count * PITCH + 8
     return call(
-        back_kernel,
-        shape(ROWS_LOC, COLS, CH, dtype=jnp.bfloat16),
+        functools.partial(back_kernel, start),
+        shape(count, COLS, CH, dtype=jnp.bfloat16),
         scratch=[VMEM((rows, CH), jnp.float32)] * 3,
         n_in=2,
         flops=1 << 30,
@@ -417,12 +417,19 @@
     tables = prepare(disc_weight, disc_head, lpips_weight, lpips_lin, out_weight)
     tile = lax.axis_index(ROWS).astype(jnp.int32).reshape(1)
     recon, grad_pre, pieces = tile_step(tile, near, own, far, conv_weight, *tables)
-    grad_features = back_step(grad_pre, conv_weight)
+    grad_1 = back_step(0, 1, grad_pre, conv_weight)
     pieces = swap(pieces.reshape(32, 2 * BLOCK, CH), ("y", "x", "core"))
+    pieces, grad_1 = lax.optimization_barrier((pieces, grad_1))
     pieces = call(first_sum_kernel, shape(16, PADDED, CH, dtype=jnp.bfloat16), name="sum_1")(pieces)
+    pieces, grad_pre = lax.optimization_barrier((pieces, grad_pre))
+    grad_2 = back_step(1, 1, grad_pre, conv_weight)
     pieces = swap(pieces, ("zh", "zl"))
+    pieces, grad_2 = lax.optimization_barrier((pieces, grad_2))
     pieces = call(second_sum_kernel, shape(8, PADDED, CH), name="sum_2")(pieces)
+    pieces, grad_pre = lax.optimization_barrier((pieces, grad_pre))
+    grad_3 = back_step(2, 2, grad_pre, conv_weight)
     pieces = swap(pieces, ("x", "core"))
+    grad_features = jnp.concatenate([grad_1, grad_2, grad_3], axis=0)
     grad_conv, grad_out = call(last_kernel, (shape(144, CH), shape(3, 16)), name="join")(pieces)
     return (
         jnp.transpose(recon, (1, 2, 0))[None],

time: 72.4 us -> 74.6 us (1.030)
  blocking collectives: 42.6 us -> 0 us
  starting transfers between devices: 15.2 us -> 36.8 us
  waiting for transfers between devices: 3.52 us -> 25.1 us
    all_to_all x2 -> x0, blocking collectives: 42.6 us -> none  [swap(): return lax.all_to_all(array, axes, split_axis=0, concat_axis=0, tiled=True)]
    all_to_all x1 -> x3, waiting for transfers between devices: 3.52 us -> 25.1 us  [swap(): return lax.all_to_all(array, axes, split_axis=0, concat_axis=0, tiled=True)]
    all_to_all x1 -> x3, starting transfers between devices: 5.79 us -> 27.3 us  [swap(): return lax.all_to_all(array, axes, split_axis=0, concat_axis=0, tiled=True)]
  transfers between devices with their start and end apart: 3 -> 5, of which waited for: 1 -> 3; matrix products, arithmetic and copies ran while one was open for 0% -> 1% of each run, Pallas kernels for 3% -> 2%
where the time goes in v4:
time: 74.6 us; the launch traced here: 74 us
  starting transfers between devices  36.8 us (49%)
  waiting for transfers between devices  25.1 us (34%)
  Pallas kernels  9.55 us (13%)
  local copies, waits for them, and re-layouts  1.05 us (1%)
  between operations  0.82 us (1%)
    all_to_all x3, starting transfers between devices, swap(): return lax.all_to_all(array, axes, split_axis=0, concat_axis=0, tiled=True)  27.3 us
    all_to_all x3, waiting for transfers between devices, swap(): return lax.all_to_all(array, axes, split_axis=0, concat_axis=0, tiled=True)  25.1 us
    ppermute x1, starting transfers between devices, body(): near = lax.ppermute(own, ROWS, swaps(range(0, TILES, 2)))  4.93 us
    pallas_call x1, Pallas kernels, tile_step(): call(main_kernel, (shape(3, ROWS_LOC, COLS), shape(N_GRAD, COLS, CH, dtyp...  4.93 us
    ppermute x1, starting transfers between devices, body(): far = lax.ppermute(own, ROWS, swaps(range(1, TILES - 1, 2)))  4.5 us
  transfers between devices with their start and end apart: 5, of which 3 were waited for; matrix products, arithmetic and copies ran while one was open for 1% of the time, Pallas kernels for 2%

profile of v4, /device:TPU:1, one launch (start us, length us, event | category | flops | bytes accessed | tf_op | source)
XLA Modules:
  0.0 74.0 jit_solution(5070969731121170598)
XLA Ops:
  0.6 0.0 copy-start.6
  0.6 0.0 copy-start.2
  0.7 0.0 copy-start.7
  0.7 1.0 %pack.1.own_ref = bf16[1088,128]{1,0:T(8,128)(2,1)S(1)} custom-call(bf16[1024,128]{1,0:T(8,128)(2,1)} %bitcast.21, f32[3,4,256]{2,1,0:T(4,128)} %bitcast.22), custom_call_target="tpu_custom_call" | custom-call | bytes 1048576 | tf_op jit(solution)/shard_map/pack/pallas_call | solution.py:323
  1.7 0.0 copy-start.1
  1.7 4.5 %collective-permute-start.1 = (bf16[1088,128]{1,0:T(8,128)(2,1)S(1)}, bf16[1088,128]{1,0:T(8,128)(2,1)S(1)}, u32[]{:S(2)}, u32[]{:S(2)}) collective-permute-start(bf16[1088,128]{1,0:T(8,128)(2,1)S(1)} %pack.1.own_ref), channel_id=1, source_target_pairs={{1,2},{2,1},{3,4},{4,3},{5,6},{6,5},{7,8},{8,7},{9,10},{10,9},{11,... | collective-permute-start | bytes 835592 | tf_op jit(solution)/shard_map/ppermute | solution.py:416
  6.2 4.9 %collective-permute-start = (bf16[1088,128]{1,0:T(8,128)(2,1)S(1)}, bf16[1088,128]{1,0:T(8,128)(2,1)S(1)}, u32[]{:S(2)}, u32[]{:S(2)}) collective-permute-start(bf16[1088,128]{1,0:T(8,128)(2,1)S(1)} %pack.1.own_ref), channel_id=1, source_target_pairs={{0,1},{1,0},{2,3},{3,2},{4,5},{5,4},{6,7},{7,6},{8,9},{9,8},{10,11... | collective-permute-start | bytes 835592 | tf_op jit(solution)/shard_map/ppermute | solution.py:415
  11.1 0.0 copy-start.5
  11.2 0.0 copy-start.3
  11.2 0.0 copy-start.4
  11.2 0.0 copy-done.6
  11.2 0.0 copy-done.2
  11.2 0.0 copy-done.7
  11.2 0.0 copy-done.1
  11.2 0.6 copy-done.5
  11.8 0.0 copy-done.3
  11.8 0.0 copy-done.4
  11.8 0.0 copy-start
  11.9 0.5 bands.1
  12.4 0.0 collective-permute-done.1.far_ref
  12.4 0.0 collective-permute-done.near_ref
  12.4 0.4 copy-done
  12.8 4.9 %tile.1 = (f32[3,4,256]{2,1,0:T(4,128)}, bf16[6,256,128]{2,1,0:T(8,128)(2,1)S(1)}, bf16[1280,128]{1,0:T(8,128)(2,1)}) custom-call(s32[1]{0:T(128)} %bitcast.tile_ref, bf16[1088,128]{1,0:T(8,128)(2,1)S(1)} %collective-permute-done.near_ref, bf16[1088,128]{1,0:T(8,128)(2,1)S(1)} %pack.1.own_ref, bf16[1088,128]{1,0:T(8,128)(2,1)S(1)} %collective-permute-done.1.far_ref, ...), custom_call_target="tpu_custom_call" | custom-call | flops 2147483648 | bytes 1048576 | tf_op jit(solution)/shard_map/tile/pallas_call | solution.py:360
  17.7 6.6 %all-to-all-start = ((bf16[32,40,128]{2,1,0:T(8,128)(2,1)}), bf16[32,40,128]{2,1,0:T(8,128)(2,1)S(1)}, u32[]{:S(2)}, u32[]{:S(2)}) async-start(bf16[32,40,128]{2,1,0:T(8,128)(2,1)} %bitcast.9), calls=%async_computation | async-start | bytes 655360 | tf_op jit(solution)/shard_map/all_to_all | solution.py:401
  24.4 0.3 features_back.3
  24.7 9.2 %all-to-all-done.in_ref = bf16[32,40,128]{2,1,0:T(8,128)(2,1)S(1)} async-done(((bf16[32,40,128]{2,1,0:T(8,128)(2,1)}), bf16[32,40,128]{2,1,0:T(8,128)(2,1)S(1)}, u32[]{:S(2)}, u32[]{:S(2)}) %all-to-all-start) | async-done | bytes 327712 | tf_op jit(solution)/shard_map/all_to_all | solution.py:401
  33.9 0.7 sum_1.1
  34.6 14.9 %all-to-all-start.1 = ((bf16[16,24,128]{2,1,0:T(8,128)(2,1)}), bf16[16,24,128]{2,1,0:T(8,128)(2,1)S(1)}, u32[]{:S(2)}, u32[]{:S(2)}) async-start(bf16[16,24,128]{2,1,0:T(8,128)(2,1)} %sum_1.1), calls=%async_computation.1 | async-start | bytes 196608 | tf_op jit(solution)/shard_map/all_to_all | solution.py:401
  49.5 0.3 features_back.4
  49.8 11.6 %all-to-all-done.1.in_ref = bf16[16,24,128]{2,1,0:T(8,128)(2,1)S(1)} async-done(((bf16[16,24,128]{2,1,0:T(8,128)(2,1)}), bf16[16,24,128]{2,1,0:T(8,128)(2,1)S(1)}, u32[]{:S(2)}, u32[]{:S(2)}) %all-to-all-start.1) | async-done | bytes 98336 | tf_op jit(solution)/shard_map/all_to_all | solution.py:401
  61.4 0.7 sum_2.1
  62.1 0.4 features_back.5
  62.6 5.8 %all-to-all-start.2 = ((f32[8,24,128]{2,1,0:T(8,128)}), f32[8,24,128]{2,1,0:T(8,128)S(1)}, u32[]{:S(2)}, u32[]{:S(2)}) async-start(f32[8,24,128]{2,1,0:T(8,128)} %sum_2.1), calls=%async_computation.2 | async-start | bytes 196608 | tf_op jit(solution)/shard_map/all_to_all | solution.py:401
  68.4 0.7 maximum_bitcast_fusion
  69.1 4.3 %all-to-all-done.2.in_ref = f32[8,24,128]{2,1,0:T(8,128)S(1)} async-done(((f32[8,24,128]{2,1,0:T(8,128)}), f32[8,24,128]{2,1,0:T(8,128)S(1)}, u32[]{:S(2)}, u32[]{:S(2)}) %all-to-all-start.2) | async-done | bytes 98336 | tf_op jit(solution)/shard_map/all_to_all | solution.py:401
  73.4 0.6 join.1
Async XLA Ops:
  0.6 10.6 %copy-start.6 = (bf16[1152,32]{1,0:T(8,128)(2,1)S(1)}, bf16[1152,32]{1,0:T(8,128)(2,1)}, u32[]{:S(2)}) copy-start(bf16[1152,32]{1,0:T(8,128)(2,1)} %constant.21.clone.back_ref) | copy-start | bytes 221188
  0.6 10.6 %copy-start.2 = (f32[3,3,3,64]{3,2,1,0:T(4,128)S(1)}, f32[3,3,3,64]{3,2,1,0:T(4,128)}, u32[]{:S(2)}) copy-start(f32[3,3,3,64]{3,2,1,0:T(4,128)} %lpips_ref.1) | copy-start | bytes 20740
  0.7 10.6 %copy-start.7 = (bf16[32,2048]{1,0:T(8,128)(2,1)S(1)}, bf16[32,2048]{1,0:T(8,128)(2,1)}, u32[]{:S(2)}) copy-start(bf16[32,2048]{1,0:T(8,128)(2,1)} %constant.20.clone.ahead_ref) | copy-start | bytes 393220
  1.7 9.5 %copy-start.1 = (f32[3,3,3,64]{3,2,1,0:T(4,128)S(1)}, f32[3,3,3,64]{3,2,1,0:T(4,128)}, u32[]{:S(2)}) copy-start(f32[3,3,3,64]{3,2,1,0:T(4,128)} %disc_ref.1) | copy-start | bytes 20740
  1.7 10.7 %collective-permute-start.1 = (bf16[1088,128]{1,0:T(8,128)(2,1)S(1)}, bf16[1088,128]{1,0:T(8,128)(2,1)S(1)}, u32[]{:S(2)}, u32[]{:S(2)}) collective-permute-start(bf16[1088,128]{1,0:T(8,128)(2,1)S(1)} %pack.1.own_ref), channel_id=1, source_target_pairs={{1,2},{2,1},{3,4},{4,3},{5,6},{6,5},{7,8},{8,7},{9,10},{10,9},{11,... | collective-permute-start | bytes 835592 | tf_op jit(solution)/shard_map/ppermute | solution.py:416
  6.2 6.2 %collective-permute-start = (bf16[1088,128]{1,0:T(8,128)(2,1)S(1)}, bf16[1088,128]{1,0:T(8,128)(2,1)S(1)}, u32[]{:S(2)}, u32[]{:S(2)}) collective-permute-start(bf16[1088,128]{1,0:T(8,128)(2,1)S(1)} %pack.1.own_ref), channel_id=1, source_target_pairs={{0,1},{1,0},{2,3},{3,2},{4,5},{5,4},{6,7},{7,6},{8,9},{9,8},{10,11... | collective-permute-start | bytes 835592 | tf_op jit(solution)/shard_map/ppermute | solution.py:415
  11.1 0.7 copy-start.5
  11.2 0.7 copy-start.3
  11.2 0.7 copy-start.4
  11.8 1.0 %copy-start = (bf16[3,3,128,128]{3,2,1,0:T(8,128)(2,1)S(1)}, bf16[3,3,128,128]{3,2,1,0:T(8,128)(2,1)}, u32[]{:S(2)}) copy-start(bf16[3,3,128,128]{3,2,1,0:T(8,128)(2,1)} %conv_ref.7) | copy-start | bytes 884740
  17.7 16.1 %all-to-all-start = ((bf16[32,40,128]{2,1,0:T(8,128)(2,1)}), bf16[32,40,128]{2,1,0:T(8,128)(2,1)S(1)}, u32[]{:S(2)}, u32[]{:S(2)}) async-start(bf16[32,40,128]{2,1,0:T(8,128)(2,1)} %bitcast.9), calls=%async_computation | async-start | bytes 655360 | tf_op jit(solution)/shard_map/all_to_all | solution.py:401
  34.6 26.8 %all-to-all-start.1 = ((bf16[16,24,128]{2,1,0:T(8,128)(2,1)}), bf16[16,24,128]{2,1,0:T(8,128)(2,1)S(1)}, u32[]{:S(2)}, u32[]{:S(2)}) async-start(bf16[16,24,128]{2,1,0:T(8,128)(2,1)} %sum_1.1), calls=%async_computation.1 | async-start | bytes 196608 | tf_op jit(solution)/shard_map/all_to_all | solution.py:401
  62.6 10.8 %all-to-all-start.2 = ((f32[8,24,128]{2,1,0:T(8,128)}), f32[8,24,128]{2,1,0:T(8,128)S(1)}, u32[]{:S(2)}, u32[]{:S(2)}) async-start(f32[8,24,128]{2,1,0:T(8,128)} %sum_2.1), calls=%async_computation.2 | async-start | bytes 196608 | tf_op jit(solution)/shard_map/all_to_all | solution.py:401

commit v5 on v3

--- a/solution.py
+++ b/solution.py
@@ -77,8 +77,8 @@
 
 
 def prep_kernel(
-    disc_ref, lpips_ref, head_ref, lin_ref, out_w_ref, ahead_ref, back_ref,
-    band_ref, band_t_ref, heads_ref, wide_ref, w27_ref,
+    disc_ref, lpips_ref, head_ref, lin_ref, out_w_ref, ahead_ref, back_ref, conv_ref,
+    band_ref, band_t_ref, heads_ref, wide_ref, two_ref, w27_ref,
 ):
     w27_ref[...] = jnp.zeros_like(w27_ref)
     for a in range(3):
@@ -89,17 +89,23 @@
     size = 3 * N_GRAD * 8
     for r in range(N_LOSS):
         band = dot(w27, ahead_ref[:, r * K_BAND : (r + 1) * K_BAND], 0, 0)
-        band_ref[r * CH : (r + 1) * CH, :] = band.astype(jnp.bfloat16)
+        band_ref[r * CH : r * CH + CH // 2, :] = (0.5 * band[: CH // 2]).astype(jnp.bfloat16)
+        band_ref[r * CH + CH // 2 : (r + 1) * CH, :] = band[CH // 2 :].astype(jnp.bfloat16)
         back = dot(back_ref[r * size : (r + 1) * size, :], w27, 1, 0)
         band_t_ref[:, r * CH : (r + 1) * CH] = back.astype(jnp.bfloat16)
-    line = jnp.concatenate([-ADV_SCALE * head_ref[...], 2.0 * lin_ref[...]], axis=1)
+    line = jnp.concatenate([-0.4 * ADV_SCALE * head_ref[...], 2.0 * lin_ref[...]], axis=1)
     heads_ref[...] = jnp.broadcast_to(line, (CH, CH)).T
     wide_ref[...] = jnp.zeros_like(wide_ref)
     wide_ref[0:3, :] = out_w_ref[...].astype(jnp.float32)
+    zero = jnp.zeros((CH, CH), jnp.bfloat16)
+    for b in range(3):
+        for k in range(4):
+            two_ref[b, k * CH : (k + 1) * CH, :CH] = conv_ref[k, b] if k < 3 else zero
+            two_ref[b, k * CH : (k + 1) * CH, CH:] = conv_ref[k - 1, b] if k else zero
 
 
 def main_kernel(
-    tile_ref, near_ref, own_ref, far_ref, conv_ref, out_w_ref,
+    tile_ref, near_ref, own_ref, far_ref, two_ref, out_w_ref,
     band_ref, band_t_ref, heads_ref,
     recon_ref, grad_pre_ref, piece_ref,
     y0, y1, y2, slope, hidden, truth, dall, packed, up_ref, down_ref,
@@ -128,17 +134,15 @@
     for buf in (y0, y2):
         for j in range(N_PRE + 1):
             buf[pl.ds(j * PITCH, 8), :] = jnp.zeros((8, CH), f32)
-    weights = jnp.concatenate(
-        [jnp.concatenate([conv_ref[a, b] for a in range(3)], axis=0) for b in range(3)], axis=1
-    )
     out_w = out_w_ref[...]
     out_w16 = out_w.astype(bf16)
     image = []
-    for j in range(N_PRE):
-        lhs = jnp.concatenate([feats(j), feats(j + 1), feats(j + 2)], axis=1)
-        prod = dot(lhs, weights, 1, 0)
+    for j in range(0, N_PRE, 2):
+        lhs = jnp.concatenate([feats(j + k) for k in range(4)], axis=1)
         for b, buf in enumerate((y0, y1, y2)):
-            buf[pl.ds(j * PITCH + 8, COLS), :] = prod[:, b * CH : (b + 1) * CH]
+            prod = dot(lhs, two_ref[b], 1, 0)
+            buf[pl.ds(j * PITCH + 8, COLS), :] = prod[:, :CH]
+            buf[pl.ds((j + 1) * PITCH + 8, COLS), :] = prod[:, CH:]
     for j in range(N_PRE):
         at = j * PITCH + 8
         pre = y0[pl.ds(at - 1, COLS), :] + y1[pl.ds(at, COLS), :] + y2[pl.ds(at + 1, COLS), :]
@@ -176,29 +180,34 @@
 
     def gelu(x):
         sq = x * x
-        th = jnp.tanh(GELU_K * x * (1.0 + GELU_C * sq))
-        low = 0.5 * (1.0 + th)
-        return x * low, low, th, sq
+        th = jnp.tanh(x * (GELU_K + (GELU_K * GELU_C) * sq))
+        rise = 1.0 + th
+        return x * rise, rise, th, sq
+
+    def norm(twice):
+        mean = jnp.sum(twice * twice, axis=0, keepdims=True) * (1.0 / half)
+        return lax.rsqrt(mean + 4.0 * NORM_EPS)
 
     for r in range(N_LOSS):
-        ok = valid(r - 2)
+        inside = 2 <= r < 2 + ROWS_LOC
+        ok = 1.0 if inside else valid(r - 2)
         both = dot(band_ref[r * CH : (r + 1) * CH, :], taps_a, 1, 0)
         other = dot(band_ref[r * CH + half : (r + 1) * CH, :], taps_b, 1, 0)
         for side in range(2):
             cols = slice(side * CH, (side + 1) * CH)
             g, a, t = both[:half, cols], both[half:, cols], other[:, cols]
-            d_disc = (heads_ref[:half, :] * ok) * (0.2 + 0.8 * sigmoid(g))
-            fa, low, th, sq = gelu(a)
+            head = heads_ref[:half, :] if inside else heads_ref[:half, :] * ok
+            d_disc = head * (1.5 + jnp.tanh(g))
+            fa, rise, th, sq = gelu(a)
             fb = gelu(t)[0]
-            inv_a = lax.rsqrt(jnp.sum(fa * fa, axis=0, keepdims=True) * (1.0 / half) + NORM_EPS)
-            inv_b = lax.rsqrt(jnp.sum(fb * fb, axis=0, keepdims=True) * (1.0 / half) + NORM_EPS)
+            inv_a, inv_b = norm(fa), norm(fb)
             na = fa * inv_a
-            up = (heads_ref[half:, :] * ok) * (na - fb * inv_b)
+            up = heads_ref[half:, :] * (na - fb * inv_b)
             mean = jnp.sum(up * na, axis=0, keepdims=True) * (1.0 / half)
-            d_feat = inv_a * (up - na * mean)
-            rise = low + 0.5 * a * (1.0 - th * th) * (GELU_K * (1.0 + 3.0 * GELU_C * sq))
+            d_feat = (inv_a * ok) * (up - na * mean)
+            slant = rise + fa * (1.0 - th) * (GELU_K + (3.0 * GELU_K * GELU_C) * sq)
             dall[r * CH : r * CH + half, cols] = d_disc.astype(bf16)
-            dall[r * CH + half : (r + 1) * CH, cols] = (d_feat * rise).astype(bf16)
+            dall[r * CH + half : (r + 1) * CH, cols] = (d_feat * slant).astype(bf16)
 
     back = dot(band_t_ref[...], dall[...], 1, 0)
     n = N_GRAD * 8
@@ -228,7 +237,8 @@
         )
         rhs.append(jnp.concatenate([feats(3 + y + a) for a in range(3)], axis=1))
     lhs, rhs = jnp.concatenate(lhs, axis=0), jnp.concatenate(rhs, axis=0)
-    packed[...] = jnp.zeros_like(packed)
+    for k in range(64):
+        packed[pl.ds(k * BLOCK + 18, 2), :] = jnp.zeros((2, CH), f32)
     for b in range(3):
         grad = dot(lhs[:, b * CH : (b + 1) * CH], rhs, 0, 0)
         for a in range(3):
@@ -333,7 +343,7 @@
     )
 
 
-def prepare(disc_weight, disc_head, lpips_weight, lpips_lin, out_weight):
+def prepare(conv_weight, disc_weight, disc_head, lpips_weight, lpips_lin, out_weight):
     bf16 = jnp.bfloat16
     ahead, back = band_selectors()
     return call(
@@ -343,18 +353,19 @@
             shape(3 * N_GRAD * 8, N_LOSS * CH, dtype=bf16),
             shape(CH, CH),
             shape(8, CH),
+            shape(3, 4 * CH, 2 * CH, dtype=bf16),
         ),
         scratch=[VMEM((32, CH), jnp.float32)],
-        n_in=7,
+        n_in=8,
         flops=1 << 28,
         name="bands",
     )(
         disc_weight, lpips_weight, disc_head.reshape(1, -1), lpips_lin.reshape(1, -1),
-        out_weight.T, jnp.asarray(ahead, bf16), jnp.asarray(back, bf16),
-    )
-
-
-def tile_step(tile, near, own, far, conv_weight, band, band_t, heads, out_w):
+        out_weight.T, jnp.asarray(ahead, bf16), jnp.asarray(back, bf16), conv_weight,
+    )
+
+
+def tile_step(tile, near, own, far, band, band_t, heads, out_w, two):
     f32, bf16 = jnp.float32, jnp.bfloat16
     rows = N_PRE * PITCH + 8
     return call(
@@ -381,7 +392,7 @@
         flops=1 << 31,
         name="tile",
         vmem=20,
-    )(tile, near, own, far, conv_weight, out_w, band, band_t, heads)
+    )(tile, near, own, far, two, out_w, band, band_t, heads)
 
 
 def back_step(grad_pre, conv_weight):
@@ -414,13 +425,17 @@
     own = pack(features[0], jnp.transpose(targets[0], (2, 0, 1)))
     near = lax.ppermute(own, ROWS, swaps(range(0, TILES, 2)))
     far = lax.ppermute(own, ROWS, swaps(range(1, TILES - 1, 2)))
-    tables = prepare(disc_weight, disc_head, lpips_weight, lpips_lin, out_weight)
+    tables = prepare(
+        conv_weight, disc_weight, disc_head, lpips_weight, lpips_lin, out_weight
+    )
     tile = lax.axis_index(ROWS).astype(jnp.int32).reshape(1)
-    recon, grad_pre, pieces = tile_step(tile, near, own, far, conv_weight, *tables)
-    grad_features = back_step(grad_pre, conv_weight)
+    recon, grad_pre, pieces = tile_step(tile, near, own, far, *tables)
     pieces = swap(pieces.reshape(32, 2 * BLOCK, CH), ("y", "x", "core"))
     pieces = call(first_sum_kernel, shape(16, PADDED, CH, dtype=jnp.bfloat16), name="sum_1")(pieces)
+    pieces, grad_pre = lax.optimization_barrier((pieces, grad_pre))
+    grad_features = back_step(grad_pre, conv_weight)
     pieces = swap(pieces, ("zh", "zl"))
+    pieces, grad_features = lax.optimization_barrier((pieces, grad_features))
     pieces = call(second_sum_kernel, shape(8, PADDED, CH), name="sum_2")(pieces)
     pieces = swap(pieces, ("x", "core"))
     grad_conv, grad_out = call(last_kernel, (shape(144, CH), shape(3, 16)), name="join")(pieces)

time: 72.4 us -> 71.4 us (0.986)
  blocking collectives: 42.6 us -> 25.2 us
  starting transfers between devices: 15.2 us -> 24.3 us
  waiting for transfers between devices: 3.52 us -> 10.4 us
    all_to_all x2, blocking collectives: 42.6 us -> 25.2 us  [swap(): return lax.all_to_all(array, axes, split_axis=0, concat_axis=0, tiled=True)]
    all_to_all x1, starting transfers between devices: 5.79 us -> 14.9 us  [swap(): return lax.all_to_all(array, axes, split_axis=0, concat_axis=0, tiled=True)]
    all_to_all x1, waiting for transfers between devices: 3.52 us -> 10.4 us  [swap(): return lax.all_to_all(array, axes, split_axis=0, concat_axis=0, tiled=True)]
where the time goes in v5:
time: 71.4 us; the launch traced here: 70.9 us
  blocking collectives  25.2 us (35%)
  starting transfers between devices  24.3 us (34%)
  waiting for transfers between devices  10.4 us (15%)
  Pallas kernels  8.55 us (12%)
  local copies, waits for them, and re-layouts  1.62 us (2%)
  between operations  0.79 us (1%)
    all_to_all x2, blocking collectives, swap(): return lax.all_to_all(array, axes, split_axis=0, concat_axis=0, tiled=True)  25.2 us
    all_to_all x1, starting transfers between devices, swap(): return lax.all_to_all(array, axes, split_axis=0, concat_axis=0, tiled=True)  14.9 us
    all_to_all x1, waiting for transfers between devices, swap(): return lax.all_to_all(array, axes, split_axis=0, concat_axis=0, tiled=True)  10.4 us
    ppermute x1, starting transfers between devices, body(): near = lax.ppermute(own, ROWS, swaps(range(0, TILES, 2)))  4.93 us
    ppermute x1, starting transfers between devices, body(): far = lax.ppermute(own, ROWS, swaps(range(1, TILES - 1, 2)))  4.5 us
    pallas_call x1, Pallas kernels, tile_step(): call(main_kernel, (shape(3, ROWS_LOC, COLS), shape(N_GRAD, COLS, CH, dtyp...  4.13 us
    unnamed x16, local copies, waits for them, and re-layouts  1.62 us
    pallas_call x1, Pallas kernels, back_step(): call(back_kernel, shape(ROWS_LOC, COLS, CH, dtype=jnp.bfloat16), scratch=...  1.49 us
  transfers between devices with their start and end apart: 3, of which 1 were waited for; matrix products, arithmetic and copies ran while one was open for 0% of the time, Pallas kernels for 3%

profile of v5, /device:TPU:1, one launch (start us, length us, event | category | flops | bytes accessed | tf_op | source)
XLA Modules:
  0.0 70.9 jit_solution(13147009387021555949)
XLA Ops:
  0.6 0.0 copy-start
  0.6 0.0 copy-start.2
  0.7 0.0 copy-start.7
  0.7 1.0 %pack.1.own_ref = bf16[1088,128]{1,0:T(8,128)(2,1)S(1)} custom-call(bf16[1024,128]{1,0:T(8,128)(2,1)} %bitcast.21, f32[3,4,256]{2,1,0:T(4,128)} %bitcast.22), custom_call_target="tpu_custom_call" | custom-call | bytes 1048576 | tf_op jit(solution)/shard_map/pack/pallas_call | solution.py:333
  1.7 0.0 copy-start.1
  1.7 4.5 %collective-permute-start.1 = (bf16[1088,128]{1,0:T(8,128)(2,1)S(1)}, bf16[1088,128]{1,0:T(8,128)(2,1)S(1)}, u32[]{:S(2)}, u32[]{:S(2)}) collective-permute-start(bf16[1088,128]{1,0:T(8,128)(2,1)S(1)} %pack.1.own_ref), channel_id=1, source_target_pairs={{1,2},{2,1},{3,4},{4,3},{5,6},{6,5},{7,8},{8,7},{9,10},{10,9},{11,... | collective-permute-start | bytes 835592 | tf_op jit(solution)/shard_map/ppermute | solution.py:427
  6.2 4.9 %collective-permute-start = (bf16[1088,128]{1,0:T(8,128)(2,1)S(1)}, bf16[1088,128]{1,0:T(8,128)(2,1)S(1)}, u32[]{:S(2)}, u32[]{:S(2)}) collective-permute-start(bf16[1088,128]{1,0:T(8,128)(2,1)S(1)} %pack.1.own_ref), channel_id=1, source_target_pairs={{0,1},{1,0},{2,3},{3,2},{4,5},{5,4},{6,7},{7,6},{8,9},{9,8},{10,11... | collective-permute-start | bytes 835592 | tf_op jit(solution)/shard_map/ppermute | solution.py:426
  11.1 0.0 copy-start.5
  11.2 0.0 copy-start.3
  11.2 0.0 copy-start.4
  11.2 0.0 copy-done
  11.2 0.0 copy-done.2
  11.2 0.0 copy-done.7
  11.2 0.0 copy-done.1
  11.2 0.6 copy-done.5
  11.8 0.0 copy-done.3
  11.8 0.0 copy-done.4
  11.8 0.0 copy-start.6
  11.8 1.0 %copy-done.6 = bf16[1152,32]{1,0:T(8,128)(2,1)S(1)} copy-done((bf16[1152,32]{1,0:T(8,128)(2,1)S(1)}, bf16[1152,32]{1,0:T(8,128)(2,1)}, u32[]{:S(2)}) %copy-start.6) | copy-done | bytes 73752
  12.8 0.6 bands.1
  13.4 0.0 collective-permute-done.1.far_ref
  13.4 0.0 collective-permute-done.near_ref
  13.4 4.1 %tile.1 = (f32[3,4,256]{2,1,0:T(4,128)}, bf16[6,256,128]{2,1,0:T(8,128)(2,1)S(1)}, bf16[1280,128]{1,0:T(8,128)(2,1)S(1)}) custom-call(s32[1]{0:T(128)} %bitcast.tile_ref, bf16[1088,128]{1,0:T(8,128)(2,1)S(1)} %collective-permute-done.near_ref, bf16[1088,128]{1,0:T(8,128)(2,1)S(1)} %pack.1.own_ref, bf16[1088,128]{1,0:T(8,128)(2,1)S(1)} %collective-permute-done.1.far_ref, ...), custom_call_target="tpu_custom_call" | custom-call | flops 2147483648 | bytes 1048576 | tf_op jit(solution)/shard_map/tile/pallas_call | solution.py:371
  17.5 15.3 %all_to_all.15.in_ref = bf16[32,40,128]{2,1,0:T(8,128)(2,1)S(1)} all-to-all(bf16[32,40,128]{2,1,0:T(8,128)(2,1)S(1)} %bitcast.17), channel_id=1, replica_groups=mesh['y'=4,'zh'=2,'zl'=8,'x'=4,'core'=2] {'y','x','core'}, dimensions={0} | all-to-all | bytes 655360 | tf_op jit(solution)/shard_map/all_to_all | solution.py:412
  32.8 0.7 sum_1.1
  33.5 14.9 %all-to-all-start.1 = ((bf16[16,24,128]{2,1,0:T(8,128)(2,1)}), bf16[16,24,128]{2,1,0:T(8,128)(2,1)S(1)}, u32[]{:S(2)}, u32[]{:S(2)}) async-start(bf16[16,24,128]{2,1,0:T(8,128)(2,1)} %sum_1.1), calls=%async_computation.1 | async-start | bytes 196608 | tf_op jit(solution)/shard_map/all_to_all | solution.py:412
  48.4 1.5 %features_back.1 = bf16[4,256,128]{2,1,0:T(8,128)(2,1)} custom-call(bf16[6,256,128]{2,1,0:T(8,128)(2,1)S(1)} %get-tuple-element.27.grad_ref, bf16[3,3,128,128]{3,2,1,0:T(8,128)(2,1)S(1)} %copy-done), custom_call_target="tpu_custom_call" | custom-call | flops 1073741824 | bytes 1048576 | tf_op jit(solution)/shard_map/features_back/pallas_call | solution.py:400
  49.9 10.4 %all-to-all-done.1.in_ref = bf16[16,24,128]{2,1,0:T(8,128)(2,1)S(1)} async-done(((bf16[16,24,128]{2,1,0:T(8,128)(2,1)}), bf16[16,24,128]{2,1,0:T(8,128)(2,1)S(1)}, u32[]{:S(2)}, u32[]{:S(2)}) %all-to-all-start.1) | async-done | bytes 98336 | tf_op jit(solution)/shard_map/all_to_all | solution.py:412
  60.4 9.9 %all_to_all.16.in_ref = f32[8,24,128]{2,1,0:T(8,128)S(1)} all-to-all(f32[8,24,128]{2,1,0:T(8,128)S(1)} %sum_2.1), channel_id=1, replica_groups=mesh['y'=4,'zh'=2,'zl'=8,'x'=4,'core'=2] {'x','core'}, dimensions={0} | all-to-all | bytes 196608 | tf_op jit(solution)/shard_map/all_to_all | solution.py:412
  70.3 0.6 join.1
  (1 shorter events, 0.0 us)
Async XLA Ops:
  0.6 10.6 %copy-start = (bf16[3,3,128,128]{3,2,1,0:T(8,128)(2,1)S(1)}, bf16[3,3,128,128]{3,2,1,0:T(8,128)(2,1)}, u32[]{:S(2)}) copy-start(bf16[3,3,128,128]{3,2,1,0:T(8,128)(2,1)} %conv_ref.3) | copy-start | bytes 884740
  0.6 10.6 %copy-start.2 = (f32[3,3,3,64]{3,2,1,0:T(4,128)S(1)}, f32[3,3,3,64]{3,2,1,0:T(4,128)}, u32[]{:S(2)}) copy-start(f32[3,3,3,64]{3,2,1,0:T(4,128)} %lpips_ref.1) | copy-start | bytes 20740
  0.7 10.6 %copy-start.7 = (bf16[32,2048]{1,0:T(8,128)(2,1)S(1)}, bf16[32,2048]{1,0:T(8,128)(2,1)}, u32[]{:S(2)}) copy-start(bf16[32,2048]{1,0:T(8,128)(2,1)} %constant.20.clone.ahead_ref) | copy-start | bytes 393220
  1.7 9.5 %copy-start.1 = (f32[3,3,3,64]{3,2,1,0:T(4,128)S(1)}, f32[3,3,3,64]{3,2,1,0:T(4,128)}, u32[]{:S(2)}) copy-start(f32[3,3,3,64]{3,2,1,0:T(4,128)} %disc_ref.1) | copy-start | bytes 20740
  1.7 11.7 %collective-permute-start.1 = (bf16[1088,128]{1,0:T(8,128)(2,1)S(1)}, bf16[1088,128]{1,0:T(8,128)(2,1)S(1)}, u32[]{:S(2)}, u32[]{:S(2)}) collective-permute-start(bf16[1088,128]{1,0:T(8,128)(2,1)S(1)} %pack.1.own_ref), channel_id=1, source_target_pairs={{1,2},{2,1},{3,4},{4,3},{5,6},{6,5},{7,8},{8,7},{9,10},{10,9},{11,... | collective-permute-start | bytes 835592 | tf_op jit(solution)/shard_map/ppermute | solution.py:427
  6.2 7.2 %collective-permute-start = (bf16[1088,128]{1,0:T(8,128)(2,1)S(1)}, bf16[1088,128]{1,0:T(8,128)(2,1)S(1)}, u32[]{:S(2)}, u32[]{:S(2)}) collective-permute-start(bf16[1088,128]{1,0:T(8,128)(2,1)S(1)} %pack.1.own_ref), channel_id=1, source_target_pairs={{0,1},{1,0},{2,3},{3,2},{4,5},{5,4},{6,7},{7,6},{8,9},{9,8},{10,11... | collective-permute-start | bytes 835592 | tf_op jit(solution)/shard_map/ppermute | solution.py:426
  11.1 0.7 copy-start.5
  11.2 0.7 copy-start.3
  11.2 0.7 copy-start.4
  11.8 1.0 %copy-start.6 = (bf16[1152,32]{1,0:T(8,128)(2,1)S(1)}, bf16[1152,32]{1,0:T(8,128)(2,1)}, u32[]{:S(2)}) copy-start(bf16[1152,32]{1,0:T(8,128)(2,1)} %constant.21.clone.back_ref) | copy-start | bytes 221188
  33.5 26.8 %all-to-all-start.1 = ((bf16[16,24,128]{2,1,0:T(8,128)(2,1)}), bf16[16,24,128]{2,1,0:T(8,128)(2,1)S(1)}, u32[]{:S(2)}, u32[]{:S(2)}) async-start(bf16[16,24,128]{2,1,0:T(8,128)(2,1)} %sum_1.1), calls=%async_computation.1 | async-start | bytes 196608 | tf_op jit(solution)/shard_map/all_to_all | solution.py:412

commit v6 on v5

--- a/solution.py
+++ b/solution.py
@@ -1,8 +1,5 @@
-import functools
-
 import jax
 import jax.numpy as jnp
-import numpy as np
 from jax import lax
 from jax.experimental import pallas as pl
 from jax.experimental.pallas import tpu as pltpu
@@ -20,9 +17,11 @@
 CH = 128
 TILES = 64
 HEIGHT = ROWS_LOC * TILES
-N_PRE = 10
-N_LOSS = 8
-N_GRAD = 6
+HALO = 3
+SLAB = HALO * COLS
+N_PRE = 8
+N_LOSS = 6
+N_GRAD = 4
 PITCH = COLS + 8
 K_BAND = 256
 BLOCK = 20
@@ -30,19 +29,23 @@
 VMEM = pltpu.VMEM
 
 
-def band_selectors():
-    ahead = np.zeros((32, N_LOSS * K_BAND), np.float32)
-    back = np.zeros((N_LOSS * 3 * N_GRAD * 8, 32), np.float32)
-    for a in range(3):
-        for b in range(3):
-            for c in range(3):
-                tap = (a * 3 + b) * 3 + c
-                for r in range(N_LOSS):
-                    ahead[tap, r * K_BAND + b * N_PRE * 8 + (r + a) * 8 + c] = 1.0
-                    q = r + a - 2
-                    if 0 <= q < N_GRAD:
-                        back[r * 3 * N_GRAD * 8 + b * N_GRAD * 8 + q * 8 + c, tap] = 1.0
-    return ahead, back
+def select_ahead(r):
+    lane = lax.broadcasted_iota(jnp.int32, (32, K_BAND), 1)
+    b, j, c = lane // (N_PRE * 8), (lane // 8) % N_PRE, lane % 8
+    return chosen(lax.broadcasted_iota(jnp.int32, (32, K_BAND), 0), j - r, b, c)
+
+
+def select_back(r):
+    dims = (3 * N_GRAD * 8, 32)
+    line = lax.broadcasted_iota(jnp.int32, dims, 0)
+    b, q, c = line // (N_GRAD * 8), (line // 8) % N_GRAD, line % 8
+    return chosen(lax.broadcasted_iota(jnp.int32, dims, 1), q + 2 - r, b, c)
+
+
+def chosen(tap, a, b, c):
+    real = jnp.logical_and(jnp.logical_and(a >= 0, a < 3), jnp.logical_and(b < 3, c < 3))
+    hit = jnp.logical_and(real, tap == 9 * a + 3 * b + c)
+    return jnp.where(hit, 1.0, 0.0).astype(jnp.bfloat16)
 
 
 def dot(a, b, ca, cb):
@@ -60,24 +63,41 @@
     return jnp.where(lane == COLS - 1, 0.0, pltpu.roll(x, COLS - 1, 1))
 
 
-def pack_kernel(own_ref, truth_ref, out_ref, truth_vmem, sems):
-    copy = pltpu.make_async_copy(own_ref, out_ref.at[pl.ds(0, TILE)], sems.at[0])
-    copy.start()
-    fetch = pltpu.make_async_copy(truth_ref, truth_vmem, sems.at[1])
+def pack_kernel(tile_ref, own_ref, truth_ref, near_ref, far_ref, truth_vmem, sems):
+    first = lax.rem(tile_ref[0], 2) == 0
+    fetch = pltpu.make_async_copy(truth_ref, truth_vmem, sems.at[2])
     fetch.start()
-    fetch.wait()
-    rows = [
-        truth_vmem[c, :, h * CH : (h + 1) * CH] for c in range(3) for h in range(COLS // CH)
-    ] + [jnp.zeros((8, CH), jnp.float32)]
-    exact = jnp.concatenate(rows, axis=0)
-    high = exact.astype(jnp.bfloat16)
-    out_ref[pl.ds(TILE, 32), :] = high
-    out_ref[pl.ds(TILE + 32, 32), :] = (exact - high.astype(jnp.float32)).astype(jnp.bfloat16)
-    copy.wait()
+
+    def slabs(top_ref, bottom_ref):
+        top = pltpu.make_async_copy(
+            own_ref.at[pl.ds(0, SLAB)], top_ref.at[pl.ds(0, SLAB)], sems.at[0]
+        )
+        bottom = pltpu.make_async_copy(
+            own_ref.at[pl.ds(COLS, SLAB)], bottom_ref.at[pl.ds(0, SLAB)], sems.at[1]
+        )
+        top.start()
+        bottom.start()
+        fetch.wait()
+        rows = [
+            truth_vmem[c, :, h * CH : (h + 1) * CH] for c in range(3) for h in range(COLS // CH)
+        ] + [jnp.zeros((8, CH), jnp.float32)]
+        high = jnp.concatenate(rows, axis=0).astype(jnp.bfloat16)
+        near_ref[pl.ds(SLAB, 32), :] = high
+        far_ref[pl.ds(SLAB, 32), :] = high
+        top.wait()
+        bottom.wait()
+
+    @pl.when(first)
+    def _():
+        slabs(far_ref, near_ref)
+
+    @pl.when(jnp.logical_not(first))
+    def _():
+        slabs(near_ref, far_ref)
 
 
 def prep_kernel(
-    disc_ref, lpips_ref, head_ref, lin_ref, out_w_ref, ahead_ref, back_ref, conv_ref,
+    disc_ref, lpips_ref, head_ref, lin_ref, out_w_ref, conv_ref,
     band_ref, band_t_ref, heads_ref, wide_ref, two_ref, w27_ref,
 ):
     w27_ref[...] = jnp.zeros_like(w27_ref)
@@ -86,12 +106,11 @@
             pair = jnp.concatenate([disc_ref[a, b], lpips_ref[a, b]], axis=1)
             w27_ref[pl.ds((a * 3 + b) * 3, 3), :] = pair
     w27 = w27_ref[...].astype(jnp.bfloat16)
-    size = 3 * N_GRAD * 8
     for r in range(N_LOSS):
-        band = dot(w27, ahead_ref[:, r * K_BAND : (r + 1) * K_BAND], 0, 0)
+        band = dot(w27, select_ahead(r), 0, 0)
         band_ref[r * CH : r * CH + CH // 2, :] = (0.5 * band[: CH // 2]).astype(jnp.bfloat16)
         band_ref[r * CH + CH // 2 : (r + 1) * CH, :] = band[CH // 2 :].astype(jnp.bfloat16)
-        back = dot(back_ref[r * size : (r + 1) * size, :], w27, 1, 0)
+        back = dot(select_back(r), w27, 1, 0)
         band_t_ref[:, r * CH : (r + 1) * CH] = back.astype(jnp.bfloat16)
     line = jnp.concatenate([-0.4 * ADV_SCALE * head_ref[...], 2.0 * lin_ref[...]], axis=1)
     heads_ref[...] = jnp.broadcast_to(line, (CH, CH)).T
@@ -105,19 +124,21 @@
 
 
 def main_kernel(
-    tile_ref, near_ref, own_ref, far_ref, two_ref, out_w_ref,
+    tile_ref, far_ref, own_ref, truth_ref, near_ref, two_ref, out_w_ref,
     band_ref, band_t_ref, heads_ref,
-    recon_ref, grad_pre_ref, piece_ref,
+    recon_ref, grad_pre_ref, near_edge_ref, far_edge_ref, piece_ref,
     y0, y1, y2, slope, hidden, truth, dall, packed, up_ref, down_ref,
 ):
     bf16, f32 = jnp.bfloat16, jnp.float32
 
-    @pl.when(lax.rem(tile_ref[0], 2) == 0)
+    first = lax.rem(tile_ref[0], 2) == 0
+
+    @pl.when(first)
     def _():
         up_ref[...] = far_ref[...]
         down_ref[...] = near_ref[...]
 
-    @pl.when(lax.rem(tile_ref[0], 2) == 1)
+    @pl.when(jnp.logical_not(first))
     def _():
         up_ref[...] = near_ref[...]
         down_ref[...] = far_ref[...]
@@ -129,7 +150,11 @@
         return jnp.where(inside, 1.0, 0.0).astype(f32)
 
     def feats(j):
-        return (up_ref, own_ref, down_ref)[j // ROWS_LOC][pl.ds(j % ROWS_LOC * COLS, COLS), :]
+        if j < HALO:
+            return up_ref[pl.ds(j * COLS, COLS), :]
+        if j < HALO + ROWS_LOC:
+            return own_ref[pl.ds((j - HALO) * COLS, COLS), :]
+        return down_ref[pl.ds((j - HALO - ROWS_LOC) * COLS, COLS), :]
 
     for buf in (y0, y2):
         for j in range(N_PRE + 1):
@@ -148,27 +173,31 @@
         pre = y0[pl.ds(at - 1, COLS), :] + y1[pl.ds(at, COLS), :] + y2[pl.ds(at + 1, COLS), :]
         sig = sigmoid(pre)
         act = (pre * sig).astype(bf16)
-        if 2 <= j < 2 + N_GRAD:
+        seen = dot(out_w16, act, 1, 1)
+        if 2 <= j < 2 + ROWS_LOC:
             slope[j - 2] = sig * (1.0 + pre * (1.0 - sig))
-        if 3 <= j < 3 + ROWS_LOC:
-            hidden[j - 3] = act
-        image.append(dot(out_w16, act, 1, 1) * valid(j - 3))
+            hidden[j - 2] = act
+        else:
+            seen = seen * valid(j - 2)
+        image.append(seen)
     for j in range(ROWS_LOC):
         for c in range(3):
-            recon_ref[c, j : j + 1, :] = image[j + 3][c : c + 1, :]
+            recon_ref[c, j : j + 1, :] = image[j + 2][c : c + 1, :]
     image = jnp.concatenate(image, axis=0)
 
     truth[...] = jnp.zeros_like(truth)
-    targets = [
-        ref[pl.ds(TILE, 32), :].astype(f32) + ref[pl.ds(TILE + 32, 32), :].astype(f32)
-        for ref in (up_ref, own_ref, down_ref)
-    ]
-    for j in range(N_PRE):
-        src, row = targets[(j + 1) // ROWS_LOC], (j + 1) % ROWS_LOC
+    for k, ref in ((-1, up_ref), (1, down_ref)):
+        rows = ref[pl.ds(SLAB, 32), :].astype(f32)
+        for y in range(2):
+            row, j = (y + 2, y) if k < 0 else (y, y + 6)
+            for c in range(3):
+                for h in range(COLS // CH):
+                    at = (c * 2 + h) * ROWS_LOC + row
+                    truth[j * 8 + c : j * 8 + c + 1, h * CH : (h + 1) * CH] = rows[at : at + 1]
+    for y in range(ROWS_LOC):
         for c in range(3):
-            for h in range(COLS // CH):
-                at = (c * 2 + h) * ROWS_LOC + row
-                truth[j * 8 + c : j * 8 + c + 1, h * CH : (h + 1) * CH] = src[at : at + 1]
+            at = (y + 2) * 8 + c
+            truth[at : at + 1, :] = truth_ref[c, y : y + 1, :]
     true_image = truth[...]
 
     def taps(x):
@@ -189,8 +218,8 @@
         return lax.rsqrt(mean + 4.0 * NORM_EPS)
 
     for r in range(N_LOSS):
-        inside = 2 <= r < 2 + ROWS_LOC
-        ok = 1.0 if inside else valid(r - 2)
+        inside = 1 <= r < 1 + ROWS_LOC
+        ok = 1.0 if inside else valid(r - 1)
         both = dot(band_ref[r * CH : (r + 1) * CH, :], taps_a, 1, 0)
         other = dot(band_ref[r * CH + half : (r + 1) * CH, :], taps_b, 1, 0)
         for side in range(2):
@@ -219,15 +248,24 @@
     out_w2 = jnp.concatenate([out_w, out_w], axis=0).astype(bf16)
     grad_out = jnp.zeros((16, CH), f32)
     for q in range(N_GRAD):
-        g = grad_image[q * 8 : (q + 1) * 8] * valid(q - 1)
+        g = grad_image[q * 8 : (q + 1) * 8]
         high = g.astype(bf16).astype(f32)
         pair = jnp.concatenate([high, g - high], axis=0)
         grad_pre = dot(pair.T.astype(bf16), out_w2, 1, 0) * slope[q]
         grad_pre_ref[q] = grad_pre.astype(bf16)
-        if 1 <= q <= ROWS_LOC:
-            y0[pl.ds((q - 1) * PITCH + 8, COLS), :] = grad_pre
-            grad_out = grad_out + dot(pair.astype(bf16), hidden[q - 1], 1, 0)
+        y0[pl.ds(q * PITCH + 8, COLS), :] = grad_pre
+        grad_out = grad_out + dot(pair.astype(bf16), hidden[q], 1, 0)
     grad_out = grad_out[:8] + grad_out[8:]
+
+    @pl.when(first)
+    def _():
+        far_edge_ref[...] = grad_pre_ref[0]
+        near_edge_ref[...] = grad_pre_ref[ROWS_LOC - 1]
+
+    @pl.when(jnp.logical_not(first))
+    def _():
+        near_edge_ref[...] = grad_pre_ref[0]
+        far_edge_ref[...] = grad_pre_ref[ROWS_LOC - 1]
 
     lhs, rhs = [], []
     for y in range(ROWS_LOC):
@@ -235,7 +273,7 @@
         lhs.append(
             jnp.concatenate([y0[pl.ds(at + 1 - b, COLS), :] for b in range(3)], axis=1).astype(bf16)
         )
-        rhs.append(jnp.concatenate([feats(3 + y + a) for a in range(3)], axis=1))
+        rhs.append(jnp.concatenate([feats(2 + y + a) for a in range(3)], axis=1))
     lhs, rhs = jnp.concatenate(lhs, axis=0), jnp.concatenate(rhs, axis=0)
     for k in range(64):
         packed[pl.ds(k * BLOCK + 18, 2), :] = jnp.zeros((2, CH), f32)
@@ -261,8 +299,21 @@
     piece_ref[...] = packed[...].astype(bf16)
 
 
-def back_kernel(grad_ref, conv_ref, out_ref, z0, z1, z2):
+def back_kernel(tile_ref, grad_ref, far_ref, near_ref, conv_ref, out_ref, z0, z1, z2, wide_ref):
     bf16, f32 = jnp.bfloat16, jnp.float32
+    first = lax.rem(tile_ref[0], 2) == 0
+    wide_ref[1 : 1 + ROWS_LOC] = grad_ref[...]
+
+    @pl.when(first)
+    def _():
+        wide_ref[0] = far_ref[...]
+        wide_ref[ROWS_LOC + 1] = near_ref[...]
+
+    @pl.when(jnp.logical_not(first))
+    def _():
+        wide_ref[0] = near_ref[...]
+        wide_ref[ROWS_LOC + 1] = far_ref[...]
+
     for buf in (z0, z2):
         for y in range(ROWS_LOC + 1):
             buf[pl.ds(y * PITCH, 8), :] = jnp.zeros((8, CH), f32)
@@ -270,7 +321,7 @@
         [jnp.concatenate([conv_ref[a, b] for a in range(3)], axis=1) for b in range(3)], axis=0
     )
     for y in range(ROWS_LOC):
-        lhs = jnp.concatenate([grad_ref[y + 2 - a] for a in range(3)], axis=1)
+        lhs = jnp.concatenate([wide_ref[y + 2 - a] for a in range(3)], axis=1)
         prod = dot(lhs, weights, 1, 1)
         for b, buf in enumerate((z0, z1, z2)):
             buf[pl.ds(y * PITCH + 8, COLS), :] = prod[:, b * CH : (b + 1) * CH]
@@ -306,7 +357,7 @@
         out_ref[c : c + 1, :] = in_ref[c, 18:19, :16]
 
 
-def call(kernel, out_shape, scratch=(), smem=0, whole=0, n_in=1, flops=0, name=None, vmem=4):
+def call(kernel, out_shape, scratch=(), smem=0, whole=0, n_in=1, flops=0, vmem=4):
     specs = [pl.BlockSpec(memory_space=pltpu.SMEM)] * smem
     specs += [pl.BlockSpec(memory_space=pltpu.HBM)] * whole
     specs += [pl.BlockSpec(memory_space=VMEM)] * (n_in - smem - whole)
@@ -321,7 +372,6 @@
         scratch_shapes=list(scratch),
         cost_estimate=pl.CostEstimate(flops=flops, bytes_accessed=1 << 20, transcendentals=0),
         compiler_params=pltpu.CompilerParams(vmem_limit_bytes=vmem << 20),
-        name=name,
     )
 
 
@@ -329,23 +379,24 @@
     return jax.ShapeDtypeStruct(dims, dtype)
 
 
-def pack(features, targets):
+def pack(tile, features, targets):
+    out = shape(SLAB + 32, CH, dtype=jnp.bfloat16)
     return call(
         pack_kernel,
-        shape(TILE + 64, CH, dtype=jnp.bfloat16),
-        scratch=[VMEM((3, ROWS_LOC, COLS), jnp.float32), pltpu.SemaphoreType.DMA((2,))],
-        n_in=2,
+        (out, out),
+        scratch=[VMEM((3, ROWS_LOC, COLS), jnp.float32), pltpu.SemaphoreType.DMA((3,))],
+        smem=1,
+        n_in=3,
         whole=2,
-        name="pack",
     )(
-        pltpu.with_memory_space_constraint(features.reshape(TILE, CH), pltpu.HBM),
+        tile,
+        pltpu.with_memory_space_constraint(features, pltpu.HBM),
         pltpu.with_memory_space_constraint(targets, pltpu.HBM),
     )
 
 
 def prepare(conv_weight, disc_weight, disc_head, lpips_weight, lpips_lin, out_weight):
     bf16 = jnp.bfloat16
-    ahead, back = band_selectors()
     return call(
         prep_kernel,
         (
@@ -356,23 +407,24 @@
             shape(3, 4 * CH, 2 * CH, dtype=bf16),
         ),
         scratch=[VMEM((32, CH), jnp.float32)],
-        n_in=8,
+        n_in=6,
         flops=1 << 28,
-        name="bands",
     )(
         disc_weight, lpips_weight, disc_head.reshape(1, -1), lpips_lin.reshape(1, -1),
-        out_weight.T, jnp.asarray(ahead, bf16), jnp.asarray(back, bf16), conv_weight,
-    )
-
-
-def tile_step(tile, near, own, far, band, band_t, heads, out_w, two):
+        out_weight.T, conv_weight,
+    )
+
+
+def tile_step(tile, far, own, truth, near, band, band_t, heads, out_w, two):
     f32, bf16 = jnp.float32, jnp.bfloat16
     rows = N_PRE * PITCH + 8
     return call(
         main_kernel,
         (
             shape(3, ROWS_LOC, COLS),
-            shape(N_GRAD, COLS, CH, dtype=bf16),
+            shape(ROWS_LOC, COLS, CH, dtype=bf16),
+            shape(COLS, CH, dtype=bf16),
+            shape(COLS, CH, dtype=bf16),
             shape(32 * 2 * BLOCK, CH, dtype=bf16),
         ),
         scratch=[
@@ -384,28 +436,28 @@
             VMEM((N_PRE * 8, COLS), f32),
             VMEM((N_LOSS * CH, COLS), bf16),
             VMEM((32 * 2 * BLOCK, CH), f32),
-            VMEM((TILE + 64, CH), bf16),
-            VMEM((TILE + 64, CH), bf16),
+            VMEM((SLAB + 32, CH), bf16),
+            VMEM((SLAB + 32, CH), bf16),
         ],
         smem=1,
-        n_in=9,
+        n_in=10,
         flops=1 << 31,
-        name="tile",
         vmem=20,
-    )(tile, near, own, far, two, out_w, band, band_t, heads)
-
-
-def back_step(grad_pre, conv_weight):
+    )(tile, far, own, truth, near, two, out_w, band, band_t, heads)
+
+
+def back_step(tile, grad_pre, far, near, conv_weight):
     rows = ROWS_LOC * PITCH + 8
     return call(
         back_kernel,
         shape(ROWS_LOC, COLS, CH, dtype=jnp.bfloat16),
-        scratch=[VMEM((rows, CH), jnp.float32)] * 3,
-        n_in=2,
+        scratch=[VMEM((rows, CH), jnp.float32)] * 3
+        + [VMEM((ROWS_LOC + 2, COLS, CH), jnp.bfloat16)],
+        smem=1,
+        n_in=5,
         flops=1 << 30,
-        name="features_back",
         vmem=8,
-    )(grad_pre, conv_weight)
+    )(tile, grad_pre, far, near, conv_weight)
 
 
 def swap(array, axes):
@@ -422,23 +474,25 @@
 def body(
     features, conv_weight, out_weight, targets, disc_weight, disc_head, lpips_weight, lpips_lin
 ):
-    own = pack(features[0], jnp.transpose(targets[0], (2, 0, 1)))
-    near = lax.ppermute(own, ROWS, swaps(range(0, TILES, 2)))
-    far = lax.ppermute(own, ROWS, swaps(range(1, TILES - 1, 2)))
+    tile = lax.axis_index(ROWS).astype(jnp.int32).reshape(1)
+    own, truth = features[0].reshape(TILE, CH), jnp.transpose(targets[0], (2, 0, 1))
+    on_chip, off_chip = swaps(range(0, TILES, 2)), swaps(range(1, TILES - 1, 2))
+    near, far = pack(tile, own, truth)
+    near, far = lax.ppermute(near, ROWS, on_chip), lax.ppermute(far, ROWS, off_chip)
     tables = prepare(
         conv_weight, disc_weight, disc_head, lpips_weight, lpips_lin, out_weight
     )
-    tile = lax.axis_index(ROWS).astype(jnp.int32).reshape(1)
-    recon, grad_pre, pieces = tile_step(tile, near, own, far, *tables)
+    recon, grad_pre, near, far, pieces = tile_step(tile, far, own, truth, near, *tables)
     pieces = swap(pieces.reshape(32, 2 * BLOCK, CH), ("y", "x", "core"))
-    pieces = call(first_sum_kernel, shape(16, PADDED, CH, dtype=jnp.bfloat16), name="sum_1")(pieces)
-    pieces, grad_pre = lax.optimization_barrier((pieces, grad_pre))
-    grad_features = back_step(grad_pre, conv_weight)
+    pieces = call(first_sum_kernel, shape(16, PADDED, CH, dtype=jnp.bfloat16))(pieces)
+    pieces, near, far = lax.optimization_barrier((pieces, near, far))
     pieces = swap(pieces, ("zh", "zl"))
+    near, far = lax.ppermute(near, ROWS, on_chip), lax.ppermute(far, ROWS, off_chip)
+    grad_features = back_step(tile, grad_pre, far, near, conv_weight)
     pieces, grad_features = lax.optimization_barrier((pieces, grad_features))
-    pieces = call(second_sum_kernel, shape(8, PADDED, CH), name="sum_2")(pieces)
+    pieces = call(second_sum_kernel, shape(8, PADDED, CH))(pieces)
     pieces = swap(pieces, ("x", "core"))
-    grad_conv, grad_out = call(last_kernel, (shape(144, CH), shape(3, 16)), name="join")(pieces)
+    grad_conv, grad_out = call(last_kernel, (shape(144, CH), shape(3, 16)))(pieces)
     return (
         jnp.transpose(recon, (1, 2, 0))[None],
         grad_features[None],

time: 71.4 us -> 70 us (0.980)
  starting transfers between devices: 24.3 us -> 28.8 us
  waiting for transfers between devices: 10.4 us -> 5.9 us
  blocking collectives: 25.2 us -> 24.3 us
    all_to_all x1, waiting for transfers between devices: 10.4 us -> 4.53 us  [swap(): return lax.all_to_all(array, axes, split_axis=0, concat_axis=0, tiled=True)]
    ppermute x2 -> x4, starting transfers between devices: 9.43 us -> 13.9 us  [the longest x2 7.08 us: body(): lax.ppermute(far, ROWS, off_chip)]
    ppermute x2 -> x4, waiting for transfers between devices: 0.01 us -> 1.37 us  [the longest x2 1.37 us: body(): lax.ppermute(far, ROWS, off_chip)]
    all_to_all x2, blocking collectives: 25.2 us -> 24.3 us  [swap(): return lax.all_to_all(array, axes, split_axis=0, concat_axis=0, tiled=True)]
  transfers between devices with their start and end apart: 3 -> 5, of which waited for: 1 -> 2; matrix products, arithmetic and copies ran while one was open for 0% -> 0% of each run, Pallas kernels for 3% -> 3%
where the time goes in v6:
time: 70 us; the launch traced here: 69.6 us
  starting transfers between devices  28.8 us (41%)
  blocking collectives  24.3 us (35%)
  Pallas kernels  7.85 us (11%)
  waiting for transfers between devices  5.9 us (8%)
  local copies, waits for them, and re-layouts  1.86 us (3%)
  between operations  0.79 us (1%)
    all_to_all x2, blocking collectives, swap(): return lax.all_to_all(array, axes, split_axis=0, concat_axis=0, tiled=True)  24.3 us
    all_to_all x1, starting transfers between devices, swap(): return lax.all_to_all(array, axes, split_axis=0, concat_axis=0, tiled=True)  14.9 us
    ppermute x2, starting transfers between devices, body(): lax.ppermute(far, ROWS, off_chip)  7.08 us
    ppermute x2, starting transfers between devices, body(): lax.ppermute(near, ROWS, on_chip)  6.84 us
    all_to_all x1, waiting for transfers between devices, swap(): return lax.all_to_all(array, axes, split_axis=0, concat_axis=0, tiled=True)  4.53 us
    pallas_call x1, Pallas kernels, tile_step(): call(main_kernel, (shape(3, ROWS_LOC, COLS), shape(ROWS_LOC, COLS, CH, dt...  3.41 us
    unnamed x16, local copies, waits for them, and re-layouts  1.86 us
    pallas_call x1, Pallas kernels, back_step(): call(back_kernel, shape(ROWS_LOC, COLS, CH, dtype=jnp.bfloat16), scratch=...  1.51 us
  transfers between devices with their start and end apart: 5, of which 2 were waited for; matrix products, arithmetic and copies ran while one was open for 0% of the time, Pallas kernels for 3%

profile of v6, /device:TPU:1, one launch (start us, length us, event | category | flops | bytes accessed | tf_op | source)
XLA Modules:
  0.0 69.6 jit_solution(14318273591268906226)
XLA Ops:
  0.6 0.0 copy-start.2
  0.6 0.0 copy-start.3
  0.7 1.1 %shard_map.111 = (bf16[800,128]{1,0:T(8,128)(2,1)S(1)}, bf16[800,128]{1,0:T(8,128)(2,1)S(1)}) custom-call(s32[1]{0:T(128)} %bitcast.tile_ref, bf16[1024,128]{1,0:T(8,128)(2,1)} %bitcast.18, f32[3,4,256]{2,1,0:T(4,128)} %bitcast.20), custom_call_target="tpu_custom_call" | custom-call | bytes 1048576 | tf_op jit(solution)/shard_map/pallas_call | solution.py:384
  1.8 4.5 %collective-permute-start = (bf16[800,128]{1,0:T(8,128)(2,1)S(1)}, bf16[800,128]{1,0:T(8,128)(2,1)S(1)}, u32[]{:S(2)}, u32[]{:S(2)}) collective-permute-start(bf16[800,128]{1,0:T(8,128)(2,1)S(1)} %get-tuple-element.23), channel_id=1, source_target_pairs={{1,2},{2,1},{3,4},{4,3},{5,6},{6,5},{7,8},{8,7},{9,10},{10,9},{11,... | collective-permute-start | bytes 614408 | tf_op jit(solution)/shard_map/ppermute | solution.py:481
  6.3 4.9 %collective-permute-start.1 = (bf16[800,128]{1,0:T(8,128)(2,1)S(1)}, bf16[800,128]{1,0:T(8,128)(2,1)S(1)}, u32[]{:S(2)}, u32[]{:S(2)}) collective-permute-start(bf16[800,128]{1,0:T(8,128)(2,1)S(1)} %get-tuple-element.24), channel_id=1, source_target_pairs={{0,1},{1,0},{2,3},{3,2},{4,5},{5,4},{6,7},{7,6},{8,9},{9,8},{10,11... | collective-permute-start | bytes 614408 | tf_op jit(solution)/shard_map/ppermute | solution.py:481
  11.2 0.0 copy-start.7
  11.2 0.0 copy-start.5
  11.2 0.0 copy-start.6
  11.2 0.0 copy-done.2
  11.3 0.0 copy-done.3
  11.3 0.6 copy-done.7
  11.9 0.0 copy-done.5
  11.9 0.0 copy-done.6
  11.9 0.0 copy-start.4
  11.9 0.7 %copy-done.4 = f32[3,3,3,64]{3,2,1,0:T(4,128)S(1)} copy-done((f32[3,3,3,64]{3,2,1,0:T(4,128)S(1)}, f32[3,3,3,64]{3,2,1,0:T(4,128)}, u32[]{:S(2)}) %copy-start.4) | copy-done | bytes 6936
  12.6 0.0 copy-start
  12.6 0.0 copy-start.1
  12.6 0.5 shard_map.112
  13.1 0.0 collective-permute-done.far_ref
  13.1 0.0 collective-permute-done.1.near_ref
  13.1 0.5 copy-done
  13.6 0.0 copy-done.1
  13.6 3.4 %shard_map.113 = (f32[3,4,256]{2,1,0:T(4,128)}, bf16[4,256,128]{2,1,0:T(8,128)(2,1)S(1)}, bf16[256,128]{1,0:T(8,128)(2,1)S(1)}, bf16[256,128]{1,0:T(8,128)(2,1)S(1)}, bf16[1280,128]{1,0:T(8,128)(2,1)S(1)}) custom-call(s32[1]{0:T(128)} %bitcast.tile_ref, bf16[800,128]{1,0:T(8,128)(2,1)S(1)} %collective-permute-done.far_ref, bf16[1024,128]{1,0:T(8,128)(2,1)S(1)} %bitcast.19, ...), custom_call_target="tpu_custom_call" | custom-call | flops 2147483648 | bytes 1048576 | tf_op jit(solution)/shard_map/pallas_call | solution.py:421
  17.0 14.5 %all_to_all.15.in_ref = bf16[32,40,128]{2,1,0:T(8,128)(2,1)S(1)} all-to-all(bf16[32,40,128]{2,1,0:T(8,128)(2,1)S(1)} %bitcast.17), channel_id=1, replica_groups=mesh['y'=4,'zh'=2,'zl'=8,'x'=4,'core'=2] {'y','x','core'}, dimensions={0} | all-to-all | bytes 655360 | tf_op jit(solution)/shard_map/all_to_all | solution.py:464
  31.5 0.7 %shard_map.114 = bf16[16,24,128]{2,1,0:T(8,128)(2,1)} custom-call(bf16[32,40,128]{2,1,0:T(8,128)(2,1)S(1)} %all_to_all.15.in_ref), custom_call_target="tpu_custom_call" | custom-call | bytes 1048576 | tf_op jit(solution)/shard_map/pallas_call | solution.py:487
  32.2 14.9 %all-to-all-start.1 = ((bf16[16,24,128]{2,1,0:T(8,128)(2,1)}), bf16[16,24,128]{2,1,0:T(8,128)(2,1)S(1)}, u32[]{:S(2)}, u32[]{:S(2)}) async-start(bf16[16,24,128]{2,1,0:T(8,128)(2,1)} %shard_map.114), calls=%async_computation.1 | async-start | bytes 196608 | tf_op jit(solution)/shard_map/all_to_all | solution.py:464
  47.1 2.6 %collective-permute-start.2 = (bf16[256,128]{1,0:T(8,128)(2,1)S(1)}, bf16[256,128]{1,0:T(8,128)(2,1)S(1)}, u32[]{:S(2)}, u32[]{:S(2)}) collective-permute-start(bf16[256,128]{1,0:T(8,128)(2,1)S(1)} %get-tuple-element.36), channel_id=1, source_target_pairs={{1,2},{2,1},{3,4},{4,3},{5,6},{6,5},{7,8},{8,7},{9,10},{10,9},{11,... | collective-permute-start | bytes 196616 | tf_op jit(solution)/shard_map/ppermute | solution.py:490
  49.7 1.9 %collective-permute-start.3 = (bf16[256,128]{1,0:T(8,128)(2,1)S(1)}, bf16[256,128]{1,0:T(8,128)(2,1)S(1)}, u32[]{:S(2)}, u32[]{:S(2)}) collective-permute-start(bf16[256,128]{1,0:T(8,128)(2,1)S(1)} %get-tuple-element.37), channel_id=1, source_target_pairs={{0,1},{1,0},{2,3},{3,2},{4,5},{5,4},{6,7},{7,6},{8,9},{9,8},{10,11... | collective-permute-start | bytes 196616 | tf_op jit(solution)/shard_map/ppermute | solution.py:490
  51.6 1.4 %collective-permute-done.2.far_ref = bf16[256,128]{1,0:T(8,128)(2,1)S(1)} collective-permute-done((bf16[256,128]{1,0:T(8,128)(2,1)S(1)}, bf16[256,128]{1,0:T(8,128)(2,1)S(1)}, u32[]{:S(2)}, u32[]{:S(2)}) %collective-permute-start.2) | collective-permute-done | bytes 65568 | tf_op jit(solution)/shard_map/ppermute | solution.py:490
  53.0 0.0 collective-permute-done.3.near_ref
  53.0 1.5 %shard_map.115 = bf16[4,256,128]{2,1,0:T(8,128)(2,1)} custom-call(s32[1]{0:T(128)} %bitcast.tile_ref, bf16[4,256,128]{2,1,0:T(8,128)(2,1)S(1)} %get-tuple-element.35.grad_ref, bf16[256,128]{1,0:T(8,128)(2,1)S(1)} %collective-permute-done.2.far_ref, bf16[256,128]{1,0:T(8,128)(2,1)S(1)} %collective-permute-done.3.near_ref, bf16[3,3,128,128]{3,2,1,0:T(8,128)(2,1)S(1)} %copy-done.2), custom_call_target="tpu_custom_call" | custom-call | flops 1073741824 | bytes 1048576 | tf_op jit(solution)/shard_map/pallas_call | solution.py:451
  54.5 4.5 %all-to-all-done.1.in_ref = bf16[16,24,128]{2,1,0:T(8,128)(2,1)S(1)} async-done(((bf16[16,24,128]{2,1,0:T(8,128)(2,1)}), bf16[16,24,128]{2,1,0:T(8,128)(2,1)S(1)}, u32[]{:S(2)}, u32[]{:S(2)}) %all-to-all-start.1) | async-done | bytes 98336 | tf_op jit(solution)/shard_map/all_to_all | solution.py:464
  59.0 9.9 %all_to_all.16.in_ref = f32[8,24,128]{2,1,0:T(8,128)S(1)} all-to-all(f32[8,24,128]{2,1,0:T(8,128)S(1)} %shard_map.116), channel_id=1, replica_groups=mesh['y'=4,'zh'=2,'zl'=8,'x'=4,'core'=2] {'x','core'}, dimensions={0} | all-to-all | bytes 196608 | tf_op jit(solution)/shard_map/all_to_all | solution.py:464
  68.9 0.6 shard_map.117
  (1 shorter events, 0.0 us)
Async XLA Ops:
  0.6 10.6 %copy-start.2 = (bf16[3,3,128,128]{3,2,1,0:T(8,128)(2,1)S(1)}, bf16[3,3,128,128]{3,2,1,0:T(8,128)(2,1)}, u32[]{:S(2)}) copy-start(bf16[3,3,128,128]{3,2,1,0:T(8,128)(2,1)} %conv_ref.3) | copy-start | bytes 884740
  0.6 10.6 %copy-start.3 = (f32[3,3,3,64]{3,2,1,0:T(4,128)S(1)}, f32[3,3,3,64]{3,2,1,0:T(4,128)}, u32[]{:S(2)}) copy-start(f32[3,3,3,64]{3,2,1,0:T(4,128)} %disc_ref.1) | copy-start | bytes 20740
  1.8 11.3 %collective-permute-start = (bf16[800,128]{1,0:T(8,128)(2,1)S(1)}, bf16[800,128]{1,0:T(8,128)(2,1)S(1)}, u32[]{:S(2)}, u32[]{:S(2)}) collective-permute-start(bf16[800,128]{1,0:T(8,128)(2,1)S(1)} %get-tuple-element.23), channel_id=1, source_target_pairs={{1,2},{2,1},{3,4},{4,3},{5,6},{6,5},{7,8},{8,7},{9,10},{10,9},{11,... | collective-permute-start | bytes 614408 | tf_op jit(solution)/shard_map/ppermute | solution.py:481
  6.3 6.8 %collective-permute-start.1 = (bf16[800,128]{1,0:T(8,128)(2,1)S(1)}, bf16[800,128]{1,0:T(8,128)(2,1)S(1)}, u32[]{:S(2)}, u32[]{:S(2)}) collective-permute-start(bf16[800,128]{1,0:T(8,128)(2,1)S(1)} %get-tuple-element.24), channel_id=1, source_target_pairs={{0,1},{1,0},{2,3},{3,2},{4,5},{5,4},{6,7},{7,6},{8,9},{9,8},{10,11... | collective-permute-start | bytes 614408 | tf_op jit(solution)/shard_map/ppermute | solution.py:481
  11.2 0.7 copy-start.7
  11.2 0.7 copy-start.5
  11.2 0.7 copy-start.6
  11.9 0.7 %copy-start.4 = (f32[3,3,3,64]{3,2,1,0:T(4,128)S(1)}, f32[3,3,3,64]{3,2,1,0:T(4,128)}, u32[]{:S(2)}) copy-start(f32[3,3,3,64]{3,2,1,0:T(4,128)} %lpips_ref.1) | copy-start | bytes 20740
  12.6 0.9 %copy-start = (bf16[1,4,256,128]{3,2,1,0:T(8,128)(2,1)S(1)}, bf16[1,4,256,128]{3,2,1,0:T(8,128)(2,1)}, u32[]{:S(2)}) copy-start(bf16[1,4,256,128]{3,2,1,0:T(8,128)(2,1)} %param.8) | copy-start | bytes 786436
  12.6 1.0 %copy-start.1 = (f32[1,4,256,3]{2,1,3,0:T(4,128)S(1)}, f32[1,4,256,3]{2,1,3,0:T(4,128)}, u32[]{:S(2)}) copy-start(f32[1,4,256,3]{2,1,3,0:T(4,128)} %param.11) | copy-start | bytes 36868
  32.2 26.8 %all-to-all-start.1 = ((bf16[16,24,128]{2,1,0:T(8,128)(2,1)}), bf16[16,24,128]{2,1,0:T(8,128)(2,1)S(1)}, u32[]{:S(2)}, u32[]{:S(2)}) async-start(bf16[16,24,128]{2,1,0:T(8,128)(2,1)} %shard_map.114), calls=%async_computation.1 | async-start | bytes 196608 | tf_op jit(solution)/shard_map/all_to_all | solution.py:464
  47.1 5.9 %collective-permute-start.2 = (bf16[256,128]{1,0:T(8,128)(2,1)S(1)}, bf16[256,128]{1,0:T(8,128)(2,1)S(1)}, u32[]{:S(2)}, u32[]{:S(2)}) collective-permute-start(bf16[256,128]{1,0:T(8,128)(2,1)S(1)} %get-tuple-element.36), channel_id=1, source_target_pairs={{1,2},{2,1},{3,4},{4,3},{5,6},{6,5},{7,8},{8,7},{9,10},{10,9},{11,... | collective-permute-start | bytes 196616 | tf_op jit(solution)/shard_map/ppermute | solution.py:490
  49.7 3.3 %collective-permute-start.3 = (bf16[256,128]{1,0:T(8,128)(2,1)S(1)}, bf16[256,128]{1,0:T(8,128)(2,1)S(1)}, u32[]{:S(2)}, u32[]{:S(2)}) collective-permute-start(bf16[256,128]{1,0:T(8,128)(2,1)S(1)} %get-tuple-element.37), channel_id=1, source_target_pairs={{0,1},{1,0},{2,3},{3,2},{4,5},{5,4},{6,7},{7,6},{8,9},{9,8},{10,11... | collective-permute-start | bytes 196616 | tf_op jit(solution)/shard_map/ppermute | solution.py:490
